TPU v7x, 512 devices: a whole 4x8x8 slice. The times are simulated.
512 devices in a mesh: dp: 64 (over z_lo, y, x), tensor: 8 (over z_hi, core).
Axes of the slice: x: 4, y: 8, z: 8 (z_hi: 4, z_lo: 2; z = z_hi * 2 + z_lo), core: 2. Of those that a mesh axis runs over, the one named last changes fastest.
Arguments:
- tokens: bfloat16 [8192, 6144], P('dp', 'tensor'), may hold values from -6 to 6
- cotangent: bfloat16 [8192, 6144], P('dp', 'tensor'), may hold values from -6 to 6
- w_gate: bfloat16 [1, 6144, 16384], P(None, 'tensor', 'dp'), may hold values from -0.078125 to 0.078125
- w_up: bfloat16 [1, 6144, 16384], P(None, 'tensor', 'dp'), may hold values from -0.078125 to 0.078125
- w_down: bfloat16 [1, 16384, 6144], P(None, 'dp', 'tensor'), may hold values from -0.046875 to 0.046875
- slot_token: int32 [64, 1, 6], P('dp'), may hold values from -1 to 127, as said below
- route_weight: float32 [64, 1, 6], P('dp'), may hold values from 0.2 to 1
Outputs:
- mixed: bfloat16 [8192, 6144], P('dp', 'tensor')
- grad_tokens: bfloat16 [8192, 6144], P('dp', 'tensor')
- grad_gate: bfloat16 [1, 6144, 16384], P(None, 'tensor', 'dp')
- grad_up: bfloat16 [1, 6144, 16384], P(None, 'tensor', 'dp')
- grad_down: bfloat16 [1, 16384, 6144], P(None, 'dp', 'tensor')
Inputs may be any that keep to these rules, and one draw needn't show every extreme that they name: `slot_token`: for each block and expert the filled slots come first and name distinct tokens of that block; every block has at least one filled slot for each expert, and for each expert some block fills all 6 slots.
All inputs are finite; a program needn't handle non-finite values.
Results may differ from a plain program's by a relative error of at most 0.0057.
Values may be sent and summed in bfloat16 or wider, within the bound.
No kernel may reach another device: no remote copies, remote signals or barrier semaphores. Data moves between devices by JAX's collectives and lax.ppermute only.
A program may use at most 64 MiB of HBM per device.

v0:
```python
import jax
import jax.numpy as jnp
from jax import lax
from jax.sharding import PartitionSpec as P


def on_device(tokens, cotangent, w_gate, w_up, w_down, slot_token, route_weight):
    tok_dev = tokens.shape[0]
    slot_ids = slot_token[0].T
    slot_weights = route_weight[0].T
    usable = slot_ids >= 0
    clipped = jnp.maximum(slot_ids, 0)
    picked = jnp.where(usable[:, :, None], tokens[clipped], 0)
    d_local = (
        slot_weights[:, :, None]
        * cotangent[clipped].astype(jnp.float32)
        * usable[:, :, None].astype(jnp.float32)
    ).astype(jnp.bfloat16)
    all_rows = lax.all_gather(picked, "dp", axis=0, tiled=True)
    gate_part = jnp.einsum("sed,edf->sef", all_rows, w_gate, preferred_element_type=jnp.float32)
    up_part = jnp.einsum("sed,edf->sef", all_rows, w_up, preferred_element_type=jnp.float32)
    gate_sum, up_sum = lax.psum((gate_part, up_part), "tensor")
    sigmoid_gate = jax.nn.sigmoid(gate_sum)
    activated = gate_sum * sigmoid_gate
    hidden = (activated * up_sum).astype(jnp.bfloat16)
    local_combine = (jnp.arange(tok_dev, dtype=jnp.int32)[:, None, None] == slot_ids[None]).astype(
        jnp.float32
    )
    own_rows = lax.psum_scatter(
        jnp.einsum("sef,efd->sed", hidden, w_down, preferred_element_type=jnp.float32),
        "dp",
        scatter_dimension=0,
        tiled=True,
    )
    mixed = jnp.einsum(
        "tce,ced->td", local_combine * slot_weights[None], own_rows, precision=lax.Precision.HIGHEST
    )
    all_grads = lax.all_gather(d_local, "dp", axis=0, tiled=True)
    hidden_part = jnp.einsum("sed,efd->sef", all_grads, w_down, preferred_element_type=jnp.float32)
    hidden_grad = lax.psum(hidden_part, "tensor")
    d_gate = (hidden_grad * up_sum * sigmoid_gate * (1.0 + gate_sum * (1.0 - sigmoid_gate))).astype(
        jnp.bfloat16
    )
    d_up = (hidden_grad * activated).astype(jnp.bfloat16)
    grad_down = jnp.einsum(
        "sef,sed->efd", hidden, all_grads, preferred_element_type=jnp.float32
    ).astype(jnp.bfloat16)
    grad_gate = jnp.einsum(
        "sed,sef->edf", all_rows, d_gate, preferred_element_type=jnp.float32
    ).astype(jnp.bfloat16)
    grad_up = jnp.einsum("sed,sef->edf", all_rows, d_up, preferred_element_type=jnp.float32).astype(
        jnp.bfloat16
    )
    own_grads = lax.psum_scatter(
        jnp.einsum("sef,edf->sed", d_gate, w_gate, preferred_element_type=jnp.float32)
        + jnp.einsum("sef,edf->sed", d_up, w_up, preferred_element_type=jnp.float32),
        "dp",
        scatter_dimension=0,
        tiled=True,
    )
    grad_tokens = jnp.einsum(
        "tce,ced->td", local_combine, own_grads, precision=lax.Precision.HIGHEST
    )
    return (
        mixed.astype(jnp.bfloat16),
        grad_tokens.astype(jnp.bfloat16),
        grad_gate,
        grad_up,
        grad_down,
    )


def solution(mesh):
    return jax.shard_map(
        on_device,
        mesh=mesh,
        in_specs=(
            P("dp", "tensor"),
            P("dp", "tensor"),
            P(None, "tensor", "dp"),
            P(None, "tensor", "dp"),
            P(None, "dp", "tensor"),
            P("dp", None, None),
            P("dp", None, None),
        ),
        out_specs=(
            P("dp", "tensor"),
            P("dp", "tensor"),
            P(None, "tensor", "dp"),
            P(None, "tensor", "dp"),
            P(None, "dp", "tensor"),
        ),
        check_vma=False,
    )
```

profile of v0, /device:TPU:6, one launch (start us, length us, event | category | flops | bytes accessed | tf_op | source)
XLA Modules:
  0.0 1043.6 jit_solution(7480080014284035748)
XLA Ops:
  7.2 0.7 maximum_bitcast_fusion
  7.9 0.7 fusion.37
  8.6 1.5 gather_fusion.1
  10.1 0.7 fusion.30
  10.9 1.5 gather_fusion
  12.5 157.4 %all_gather.7 = bf16[384,1,768]{2,1,0:T(2,128)(2,1)S(1)} all-gather(bf16[6,1,768]{2,1,0:T(2,128)(2,1)S(1)} %copy.18), channel_id=1, replica_groups=mesh['dp'=64,'tensor'=8] {'dp'}, dimensions={0}, use_global_device_ids=true | all-gather | bytes 599040 | tf_op jit(solution)/shard_map/all_gather | solution.py:38
  169.9 158.1 %all_gather.6 = bf16[384,1,768]{2,1,0:T(2,128)(2,1)S(1)} all-gather(bf16[6,1,768]{2,1,0:T(2,128)(2,1)S(1)} %copy.16), channel_id=1, replica_groups=mesh['dp'=64,'tensor'=8] {'dp'}, dimensions={0}, use_global_device_ids=true | all-gather | bytes 599040 | tf_op jit(solution)/shard_map/all_gather | solution.py:19
  328.0 0.9 copy-done.2
  329.0 1.1 convolution_bitcast_fusion.2
  330.0 1.1 convolution_bitcast_fusion.3
  331.1 1.1 convolution_bitcast_fusion.1
  332.3 85.4 %all-reduce.9.cloned.1.call-done = (f32[384,1,256]{2,0,1:T(8,128)}, f32[384,1,256]{2,0,1:T(8,128)}, f32[384,1,256]{2,0,1:T(8,128)}) async-done(((f32[384,1,256]{2,0,1:T(8,128)}, f32[384,1,256]{2,0,1:T(8,128)}, f32[384,1,256]{2,0,1:T(8,128)}), (f32[384,1,256]{2,0,1:T(8,128)}, f32[384,1,256]{2,0,1:T(8,128)}, f32[384,1,256]{2,0,1:T(8,128)})) %all-reduce.9.cloned.1.call-update) | async-done | bytes 1179664 | tf_op jit(solution)/shard_map/psum | solution.py:22
  417.7 1.5 fusion.21
  419.1 0.4 fusion.14
  419.9 2.2 copy.19
  422.4 2.2 copy.17
  424.7 1.3 dynamic-slice
  426.6 1.1 fusion.3
  427.7 1.2 fusion.2
  428.9 1.2 fusion.1
  430.1 603.6 %all-reduce.7.cloned.1.call-done = (f32[384,1,768]{2,1,0:T(1,128)}, f32[384,1,768]{2,1,0:T(1,128)}) async-done(((f32[384,1,768]{2,1,0:T(1,128)}, f32[384,1,768]{2,1,0:T(1,128)}), (f32[384,1,768]{2,1,0:T(1,128)}, f32[384,1,768]{2,1,0:T(1,128)})) %all-reduce.7.cloned.1.call-update) | async-done | bytes 2359312
  1033.7 0.7 constant_dynamic-slice_fusion
  1034.5 1.0 convolution_convert_fusion.3
  1035.4 1.3 convolution_convert_fusion.4
  (20 shorter events, 1.0 us)
Async XLA Ops:
  7.2 322.9 %copy-start = (bf16[1,768,256]{2,1,0:T(8,128)(2,1)S(1)}, bf16[1,768,256]{2,1,0:T(8,128)(2,1)}, u32[]{:S(2)}) copy-start(bf16[1,768,256]{2,1,0:T(8,128)(2,1)} %param.9) | copy-start | bytes 1179652
  7.2 410.5 %all-reduce.9.cloned.1.call-start = ((), (), s32[]{:S(2)}) async-start(), calls=%async_computation.1 | async-start | bytes 2359296 | tf_op jit(solution)/shard_map/psum | solution.py:22
  328.0 1.0 copy-start.2
  328.9 2.1 copy-start.1
  332.2 701.5 %all-reduce.7.cloned.1.call-start = ((), (), s32[]{:S(2)}) async-start(), calls=%async_computation | async-start | bytes 4718592
  427.7 606.7 %copy-start.3 = (s32[1,1,6]{2,1,0:T(1,128)S(1)}, s32[1,1,6]{2,1,0:T(1,128)}, u32[]{:S(2)}) copy-start(s32[1,1,6]{2,1,0:T(1,128)} %param.12) | copy-start | bytes 76
  427.7 607.7 %copy-start.4 = (f32[1,1,6]{2,1,0:T(1,128)S(1)}, f32[1,1,6]{2,1,0:T(1,128)}, u32[]{:S(2)}) copy-start(f32[1,1,6]{2,1,0:T(1,128)} %param.13) | copy-start | bytes 76
Sparse Core Ops, SparseCore 0:
  332.3 85.3 all-reduce.8
  424.8 608.8 all-reduce.6
where the time goes:
time: 1040 us
  waiting for transfers between devices  689 us (66%)
  blocking collectives  315 us (30%)
  between operations  14.8 us (1%)
  local copies, waits for them, and re-layouts  10.6 us (1%)
    unnamed x3, waiting for transfers between devices  604 us
    all_gather x1, blocking collectives, on_device(): all_rows = lax.all_gather(picked, 'dp', axis=0, tiled=True)  158 us
    all_gather x1, blocking collectives, on_device(): all_grads = lax.all_gather(d_local, 'dp', axis=0, tiled=True)  157 us
    psum x1, waiting for transfers between devices, on_device(): gate_sum, up_sum = lax.psum((gate_part, up_part), 'tensor')  85.4 us
  transfers between devices with their start and end apart: 2, of which 2 were waited for; matrix products, arithmetic and copies ran while one was open for 0% of the time, Pallas kernels for 0%

commit v1 on v0

v1 whole, which is shorter than its diff:
```python
import jax
import jax.numpy as jnp
from jax import lax
from jax.sharding import Mesh
from jax.sharding import PartitionSpec as P

AXES = ("zl", "y", "x", "zh", "c")
SIZES = (2, 8, 4, 4, 2)
DP = ("zl", "y", "x")
TENSOR = ("zh", "c")
BF16 = jnp.bfloat16
F32 = jnp.float32


def exchange(pieces, axes):
    return lax.all_to_all(pieces, axes, split_axis=0, concat_axis=0, tiled=True)


def spread(piece, axes, n):
    return exchange(jnp.broadcast_to(piece[None], (n, *piece.shape)), axes)


def dot(a, b, ca, cb):
    return lax.dot_general(a, b, (((ca,), (cb,)), ((), ())), preferred_element_type=F32)


def on_device(tokens, cotangent, w_gate, w_up, w_down, slot_token, route_weight):
    w_gate, w_up, w_down = w_gate[0], w_up[0], w_down[0]
    slots, weights = slot_token[0, 0], route_weight[0, 0]
    tok, d = tokens.shape
    cap = slots.shape[0]
    ff = w_gate.shape[1]
    one_hot = (slots[:, None] == jnp.arange(tok, dtype=jnp.int32)[None, :]).astype(BF16)
    picked = dot(one_hot, tokens, 1, 0).astype(BF16)
    d_rows = (weights[:, None] * dot(one_hot, cotangent, 1, 0)).astype(BF16)

    near = spread(jnp.concatenate([picked, d_rows]), "y", 8)
    near = near.reshape(8, 2, cap, d).transpose(1, 0, 2, 3).reshape(2, 8 * cap, d)
    rows = spread(near, ("zl", "x"), 8)
    n = 64 * cap
    all_rows = rows[:, 0].reshape(n, d)
    all_grads = rows[:, 1].reshape(n, d)

    part = jnp.concatenate(
        [dot(all_rows, w_gate, 1, 0), dot(all_rows, w_up, 1, 0), dot(all_grads, w_down, 1, 1)], axis=1
    )
    part = jnp.sum(exchange(part.reshape(2, n // 2, 3 * ff), "c"), axis=0).astype(BF16)
    sums = jnp.sum(exchange(part.reshape(4, n // 8, 3 * ff), "zh").astype(F32), axis=0)
    gate_sum, up_sum, hidden_grad = sums[:, :ff], sums[:, ff : 2 * ff], sums[:, 2 * ff :]
    sigmoid_gate = jax.nn.sigmoid(gate_sum)
    activated = gate_sum * sigmoid_gate
    own = jnp.concatenate(
        [
            activated * up_sum,
            hidden_grad * up_sum * sigmoid_gate * (1.0 + gate_sum * (1.0 - sigmoid_gate)),
            hidden_grad * activated,
        ],
        axis=1,
    ).astype(BF16)
    full = spread(spread(own, "zh", 4).reshape(n // 2, 3 * ff), "c", 2).reshape(n, 3 * ff)
    hidden, d_gate, d_up = full[:, :ff], full[:, ff : 2 * ff], full[:, 2 * ff :]

    out = dot(hidden, w_down, 1, 0).astype(BF16)
    back = (dot(d_gate, w_gate, 1, 1) + dot(d_up, w_up, 1, 1)).astype(BF16)
    both = jnp.stack([out.reshape(8, 8 * cap, d), back.reshape(8, 8 * cap, d)], axis=1)
    both = jnp.sum(exchange(both, ("zl", "x")).astype(F32), axis=0).astype(BF16)
    both = both.reshape(2, 8, cap, d).transpose(1, 0, 2, 3).reshape(8, 2 * cap, d)
    both = jnp.sum(exchange(both, "y").astype(F32), axis=0)
    mixed = dot(one_hot, (weights[:, None] * both[:cap]).astype(BF16), 0, 0).astype(BF16)
    grad_tokens = dot(one_hot, both[cap:].astype(BF16), 0, 0).astype(BF16)

    grad_gate = dot(all_rows, d_gate, 0, 0).astype(BF16)
    grad_up = dot(all_rows, d_up, 0, 0).astype(BF16)
    grad_down = dot(hidden, all_grads, 0, 0).astype(BF16)
    return mixed, grad_tokens, grad_gate[None], grad_up[None], grad_down[None]


def solution(mesh):
    fine = Mesh(mesh.devices.reshape(SIZES), AXES)
    acts = P(DP, TENSOR)
    w_in = P(None, TENSOR, DP)
    w_out = P(None, DP, TENSOR)
    slot = P(DP, None, None)
    return jax.shard_map(
        on_device,
        mesh=fine,
        in_specs=(acts, acts, w_in, w_in, w_out, slot, slot),
        out_specs=(acts, acts, w_in, w_in, w_out),
        check_vma=False,
    )
```

time: 1040 us -> 130 us (0.12)
  waiting for transfers between devices: 689 us -> 22.1 us
  blocking collectives: 315 us -> 81.8 us
  between operations: 14.8 us -> 0.87 us
    unnamed x3 -> x0, waiting for transfers between devices: 604 us -> none
    all_gather x2 -> x0, blocking collectives: 315 us -> none  [the longest x1 158 us: on_device(): all_rows = lax.all_gather(picked, 'dp', axis=0, tiled=True)]
    psum x1 -> x0, waiting for transfers between devices: 85.4 us -> none  [on_device(): gate_sum, up_sum = lax.psum((gate_part, up_part), 'tensor')]
    all_to_all x0 -> x6, blocking collectives: none -> 81.8 us  [exchange(): return lax.all_to_all(pieces, axes, split_axis=0, concat_axis=0, tiled=True)]
    all_to_all x0 -> x2, waiting for transfers between devices: none -> 22.1 us  [exchange(): return lax.all_to_all(pieces, axes, split_axis=0, concat_axis=0, tiled=True)]
  transfers between devices with their start and end apart: 2 -> 2, of which waited for: 2 -> 2; matrix products, arithmetic and copies ran while one was open for 0% -> 3% of each run, Pallas kernels for 0% -> 0%
where the time goes in v1:
time: 130 us; the launch traced here: 129 us
  blocking collectives  81.8 us (63%)
  waiting for transfers between devices  22.1 us (17%)
  matrix products  9.99 us (8%)
  starting transfers between devices  8.51 us (7%)
  local copies, waits for them, and re-layouts  3.88 us (3%)
  other arithmetic  1.56 us (1%)
    all_to_all x6, blocking collectives, exchange(): return lax.all_to_all(pieces, axes, split_axis=0, concat_axis=0, tiled=True)  81.8 us
    all_to_all x2, waiting for transfers between devices, exchange(): return lax.all_to_all(pieces, axes, split_axis=0, concat_axis=0, tiled=True)  22.1 us
    dot_general x13, matrix products, dot(): lax.dot_general(a, b, (((ca,), (cb,)), ((), ())), preferred_element_type=...  9.99 us
    all_to_all x2, starting transfers between devices, exchange(): return lax.all_to_all(pieces, axes, split_axis=0, concat_axis=0, tiled=True)  8.51 us
  transfers between devices with their start and end apart: 2, of which 2 were waited for; matrix products, arithmetic and copies ran while one was open for 3% of the time, Pallas kernels for 0%

profile of v1, /device:TPU:6, one launch (start us, length us, event | category | flops | bytes accessed | tf_op | source)
XLA Modules:
  0.0 128.6 jit_solution(6242931552831911421)
XLA Ops:
  0.6 1.2 convolution_convert_fusion.6
  1.8 1.1 fusion.4
  3.0 17.4 %all_to_all.40 = bf16[8,12,768]{2,1,0:T(8,128)(2,1)S(1)} all-to-all(bf16[8,12,768]{2,1,0:T(8,128)(2,1)S(1)} %broadcast_in_dim.36), channel_id=1, replica_groups=mesh['zl'=2,'y'=8,'x'=4,'zh'=4,'c'=2] {'y'}, dimensions={0} | all-to-all | bytes 294912 | tf_op jit(solution)/shard_map/all_to_all | solution.py:16
  20.7 19.6 %all_to_all.41 = bf16[8,2,48,768]{3,2,1,0:T(8,128)(2,1)S(1)} all-to-all(bf16[8,2,48,768]{3,2,1,0:T(8,128)(2,1)S(1)} %broadcast_in_dim.38), channel_id=1, replica_groups=mesh['zl'=2,'y'=8,'x'=4,'zh'=4,'c'=2] {'zl','x'}, dimensions={0} | all-to-all | bytes 2359296 | tf_op jit(solution)/shard_map/all_to_all | solution.py:16
  40.4 0.9 copy-done.3
  41.3 0.4 fusion.9
  41.7 0.4 fusion.13
  42.2 0.4 fusion.6
  42.7 1.4 %copy.29 = f32[384,768]{1,0:T(8,128)} copy(f32[384,768]{0,1:T(8,128)S(1)} %pad_maximum_fusion) | data formatting | bytes 2359296 | tf_op jit(solution)/shard_map/concatenate | solution.py:44
  44.0 5.8 %all_to_all.42 = f32[2,192,768]{2,1,0:T(8,128)S(1)} all-to-all(f32[2,192,768]{2,1,0:T(8,128)} %bitcast.57), channel_id=1, replica_groups=mesh['zl'=2,'y'=8,'x'=4,'zh'=4,'c'=2] {'c'}, dimensions={0} | all-to-all | bytes 2359296 | tf_op jit(solution)/shard_map/all_to_all | solution.py:16
  49.9 21.3 %all_to_all.43 = bf16[4,48,768]{2,1,0:T(8,128)(2,1)S(1)} all-to-all(bf16[4,48,768]{2,1,0:T(8,128)(2,1)S(1)} %bitcast.67), channel_id=1, replica_groups=mesh['zl'=2,'y'=8,'x'=4,'zh'=4,'c'=2] {'zh'}, dimensions={0} | all-to-all | bytes 589824 | tf_op jit(solution)/shard_map/all_to_all | solution.py:16
  71.4 13.3 %all_to_all.44 = bf16[4,48,768]{2,1,0:T(8,128)(2,1)S(1)} all-to-all(bf16[4,48,768]{2,1,0:T(8,128)(2,1)S(1)} %broadcast_in_dim.39), channel_id=1, replica_groups=mesh['zl'=2,'y'=8,'x'=4,'zh'=4,'c'=2] {'zh'}, dimensions={0} | all-to-all | bytes 589824 | tf_op jit(solution)/shard_map/all_to_all | solution.py:16
  84.7 4.3 %all_to_all.45 = bf16[2,192,768]{2,1,0:T(8,128)(2,1)S(1)} all-to-all(bf16[2,192,768]{2,1,0:T(8,128)(2,1)S(1)} %broadcast_in_dim.41), channel_id=1, replica_groups=mesh['zl'=2,'y'=8,'x'=4,'zh'=4,'c'=2] {'c'}, dimensions={0} | all-to-all | bytes 1179648 | tf_op jit(solution)/shard_map/all_to_all | solution.py:16
  90.4 1.1 pad_maximum_fusion.1
  91.5 5.1 %all-to-all-start.6 = ((bf16[8,2,48,768]{3,2,1,0:T(8,128)(2,1)}), bf16[8,2,48,768]{3,2,1,0:T(8,128)(2,1)S(1)}, u32[]{:S(2)}, u32[]{:S(2)}) async-start(bf16[8,2,48,768]{3,2,1,0:T(8,128)(2,1)} %pad_maximum_fusion.1), calls=%async_computation.6 | async-start | bytes 2359296 | tf_op jit(solution)/shard_map/all_to_all | solution.py:16
  96.6 1.2 fusion.1
  97.8 14.3 %all-to-all-done.6 = bf16[8,2,48,768]{3,2,1,0:T(8,128)(2,1)S(1)} async-done(((bf16[8,2,48,768]{3,2,1,0:T(8,128)(2,1)}), bf16[8,2,48,768]{3,2,1,0:T(8,128)(2,1)S(1)}, u32[]{:S(2)}, u32[]{:S(2)}) %all-to-all-start.6) | async-done | bytes 1179680 | tf_op jit(solution)/shard_map/all_to_all | solution.py:16
  112.3 0.7 copy.35
  113.0 3.4 %all-to-all-start.7 = ((bf16[8,12,768]{2,1,0:T(8,128)(2,1)}), bf16[8,12,768]{2,1,0:T(8,128)(2,1)S(1)}, u32[]{:S(2)}, u32[]{:S(2)}) async-start(bf16[8,12,768]{2,1,0:T(8,128)(2,1)} %copy.35), calls=%async_computation.7 | async-start | bytes 393216 | tf_op jit(solution)/shard_map/all_to_all | solution.py:16
  116.5 1.1 fusion.3
  117.6 1.2 fusion.2
  118.8 7.8 %all-to-all-done.7 = bf16[8,12,768]{2,1,0:T(8,128)(2,1)S(1)} async-done(((bf16[8,12,768]{2,1,0:T(8,128)(2,1)}), bf16[8,12,768]{2,1,0:T(8,128)(2,1)S(1)}, u32[]{:S(2)}, u32[]{:S(2)}) %all-to-all-start.7) | async-done | bytes 147488 | tf_op jit(solution)/shard_map/all_to_all | solution.py:16
  126.6 1.0 convolution_convert_fusion.4
  127.6 1.0 convolution_convert_fusion.5
  (34 shorter events, 2.3 us)
Async XLA Ops:
  0.6 41.5 %copy-start = (bf16[1,256,768]{2,1,0:T(8,128)(2,1)S(1)}, bf16[1,256,768]{2,1,0:T(8,128)(2,1)}, u32[]{:S(2)}) copy-start(bf16[1,256,768]{2,1,0:T(8,128)(2,1)} %param.11) | copy-start | bytes 1179652
  40.3 1.0 copy-start.3
  40.4 1.3 %copy-start.1 = (bf16[1,768,256]{2,1,0:T(8,128)(2,1)S(1)}, bf16[1,768,256]{2,1,0:T(8,128)(2,1)}, u32[]{:S(2)}) copy-start(bf16[1,768,256]{2,1,0:T(8,128)(2,1)} %param.9) | copy-start | bytes 1179652
  84.7 4.7 %copy-start.2 = (bf16[1,768,256]{2,1,0:T(8,128)(2,1)S(1)}, bf16[1,768,256]{2,1,0:T(8,128)(2,1)}, u32[]{:S(2)}) copy-start(bf16[1,768,256]{2,1,0:T(8,128)(2,1)} %param.9) | copy-start | bytes 1179652
  89.0 1.0 copy-start.4
  91.5 20.5 %all-to-all-start.6 = ((bf16[8,2,48,768]{3,2,1,0:T(8,128)(2,1)}), bf16[8,2,48,768]{3,2,1,0:T(8,128)(2,1)S(1)}, u32[]{:S(2)}, u32[]{:S(2)}) async-start(bf16[8,2,48,768]{3,2,1,0:T(8,128)(2,1)} %pad_maximum_fusion.1), calls=%async_computation.6 | async-start | bytes 2359296 | tf_op jit(solution)/shard_map/all_to_all | solution.py:16
  113.0 13.5 %all-to-all-start.7 = ((bf16[8,12,768]{2,1,0:T(8,128)(2,1)}), bf16[8,12,768]{2,1,0:T(8,128)(2,1)S(1)}, u32[]{:S(2)}, u32[]{:S(2)}) async-start(bf16[8,12,768]{2,1,0:T(8,128)(2,1)} %copy.35), calls=%async_computation.7 | async-start | bytes 393216 | tf_op jit(solution)/shard_map/all_to_all | solution.py:16
  116.4 10.2 %copy-start.5 = (s32[1,1,6]{2,1,0:T(1,128)S(1)}, s32[1,1,6]{2,1,0:T(1,128)}, u32[]{:S(2)}) copy-start(s32[1,1,6]{2,1,0:T(1,128)} %param.12) | copy-start | bytes 76
  116.5 11.2 %copy-start.6 = (f32[1,1,6]{2,1,0:T(1,128)S(1)}, f32[1,1,6]{2,1,0:T(1,128)}, u32[]{:S(2)}) copy-start(f32[1,1,6]{2,1,0:T(1,128)} %param.13) | copy-start | bytes 76

commit v2 on v1

v2 whole, which is shorter than its diff:
```python
import jax
import jax.numpy as jnp
from jax import lax
from jax.sharding import Mesh
from jax.sharding import PartitionSpec as P

AXES = ("zl", "y", "x", "zh", "c")
SIZES = (2, 8, 4, 4, 2)
DP = ("zl", "y", "x")
TENSOR = ("zh", "c")
BF16 = jnp.bfloat16
F32 = jnp.float32


def exchange(pieces, axes):
    return lax.all_to_all(pieces, axes, split_axis=0, concat_axis=0, tiled=True)


def spread(piece, axes, n):
    return exchange(jnp.broadcast_to(piece[None], (n, *piece.shape)), axes)


def total(pieces):
    out = pieces[0].astype(F32)
    for j in range(1, pieces.shape[0]):
        out = out + pieces[j].astype(F32)
    return out


def dot(a, b, ca, cb):
    return lax.dot_general(a, b, (((ca,), (cb,)), ((), ())), preferred_element_type=F32)


def on_device(tokens, cotangent, w_gate, w_up, w_down, slot_token, route_weight):
    w_gate, w_up, w_down = w_gate[0], w_up[0], w_down[0]
    slots, weights = slot_token[0, 0], route_weight[0, 0]
    tok, d = tokens.shape
    cap = slots.shape[0]
    ff = w_gate.shape[1]
    one_hot = (slots[:, None] == jnp.arange(tok, dtype=jnp.int32)[None, :]).astype(BF16)
    picked = dot(one_hot, tokens, 1, 0).astype(BF16)
    d_rows = (weights[:, None] * dot(one_hot, cotangent, 1, 0)).astype(BF16)

    half = ff // 2
    kept_at = lax.axis_index("c").astype(jnp.uint32) * half
    sent_at = half - kept_at
    near, kept_at, sent_at = lax.optimization_barrier((jnp.concatenate([picked, d_rows]), kept_at, sent_at))
    near = spread(near, "y", 8)
    near = near.reshape(8, 2, cap, d).transpose(1, 0, 2, 3).reshape(2, 8 * cap, d)
    rows = spread(near, ("zl", "x"), 8)
    n = 64 * cap
    all_rows = rows[:, 0].reshape(n, d)
    all_grads = rows[:, 1].reshape(n, d)

    part = jnp.stack([dot(w_gate, all_rows, 0, 1), dot(w_up, all_rows, 0, 1), dot(w_down, all_grads, 1, 1)])
    sent = lax.ppermute(
        lax.dynamic_slice_in_dim(part, sent_at, half, axis=1), "c", [(0, 1), (1, 0)]
    )
    part = (lax.dynamic_slice_in_dim(part, kept_at, half, axis=1) + sent).astype(BF16)
    part = part.reshape(3, 4, ff // 8, n).transpose(1, 0, 2, 3)
    gate_sum, up_sum, hidden_grad = total(exchange(part, "zh"))
    sigmoid_gate = jax.nn.sigmoid(gate_sum)
    activated = gate_sum * sigmoid_gate
    own = jnp.stack(
        [
            activated * up_sum,
            hidden_grad * up_sum * sigmoid_gate * (1.0 + gate_sum * (1.0 - sigmoid_gate)),
            hidden_grad * activated,
        ]
    ).astype(BF16)
    full = lax.all_gather(spread(own, "zh", 4), "c", axis=0, tiled=True)
    hidden, d_gate, d_up = (full[:, i].reshape(ff, n) for i in range(3))

    out = dot(hidden, w_down, 0, 0).astype(BF16)
    back = (dot(d_gate, w_gate, 0, 1) + dot(d_up, w_up, 0, 1)).astype(BF16)
    both = jnp.stack([out.reshape(8, 8 * cap, d), back.reshape(8, 8 * cap, d)], axis=1)
    both = total(exchange(both, ("zl", "x"))).astype(BF16)
    both = both.reshape(2, 8, cap, d).transpose(1, 0, 2, 3).reshape(8, 2 * cap, d)
    both = total(exchange(both, "y"))
    mixed = dot(one_hot, (weights[:, None] * both[:cap]).astype(BF16), 0, 0).astype(BF16)
    grad_tokens = dot(one_hot, both[cap:].astype(BF16), 0, 0).astype(BF16)

    grad_gate = dot(all_rows, d_gate, 0, 1).astype(BF16)
    grad_up = dot(all_rows, d_up, 0, 1).astype(BF16)
    grad_down = dot(hidden, all_grads, 1, 0).astype(BF16)
    return mixed, grad_tokens, grad_gate[None], grad_up[None], grad_down[None]


def solution(mesh):
    fine = Mesh(mesh.devices.reshape(SIZES), AXES)
    acts = P(DP, TENSOR)
    w_in = P(None, TENSOR, DP)
    w_out = P(None, DP, TENSOR)
    slot = P(DP, None, None)
    return jax.shard_map(
        on_device,
        mesh=fine,
        in_specs=(acts, acts, w_in, w_in, w_out, slot, slot),
        out_specs=(acts, acts, w_in, w_in, w_out),
        check_vma=False,
    )
```

time: 130 us -> 129 us (level)
  blocking collectives: 81.8 us -> 73.8 us
  other arithmetic: 1.56 us -> 4.61 us
  waiting for transfers between devices: 22.1 us -> 24.1 us
  starting transfers between devices: 8.51 us -> 10.4 us
    all_to_all x6 -> x4, blocking collectives: 81.8 us -> 71.6 us  [exchange(): return lax.all_to_all(pieces, axes, split_axis=0, concat_axis=0, tiled=True)]
    another operation x1, other arithmetic: 1.12 us -> 3.71 us  [on_device(): jnp.stack([out.reshape(8, 8 * cap, d), back.reshape(8, 8 * cap, d)], axis=1)]
    all_gather x0 -> x1, blocking collectives: none -> 2.22 us  [on_device(): full = lax.all_gather(spread(own, 'zh', 4), 'c', axis=0, tiled=True)]
    another operation x0 -> x2, local copies, waits for them, and re-layouts: none -> 2.11 us  [on_device(): jnp.stack([out.reshape(8, 8 * cap, d), back.reshape(8, 8 * cap, d)], axis=1)]
    ppermute x0 -> x1, waiting for transfers between devices: none -> 1.97 us  [on_device(): lax.ppermute(lax.dynamic_slice_in_dim(part, sent_at, half, axis=1), 'c',...]
    ppermute x0 -> x1, starting transfers between devices: none -> 1.92 us  [on_device(): lax.ppermute(lax.dynamic_slice_in_dim(part, sent_at, half, axis=1), 'c',...]
    concatenate x1 -> x0, local copies, waits for them, and re-layouts: 1.38 us -> none  [on_device(): jnp.concatenate([dot(all_rows, w_gate, 1, 0), dot(all_rows, w_up, 1, 0),...]
  transfers between devices with their start and end apart: 2 -> 3, of which waited for: 2 -> 3; matrix products, arithmetic and copies ran while one was open for 3% -> 3% of each run, Pallas kernels for 0% -> 0%
where the time goes in v2:
time: 129 us; the launch traced here: 128 us
  blocking collectives  73.8 us (57%)
  waiting for transfers between devices  24.1 us (19%)
  starting transfers between devices  10.4 us (8%)
  matrix products  10 us (8%)
  other arithmetic  4.61 us (4%)
  local copies, waits for them, and re-layouts  4.29 us (3%)
    all_to_all x4, blocking collectives, exchange(): return lax.all_to_all(pieces, axes, split_axis=0, concat_axis=0, tiled=True)  71.6 us
    all_to_all x2, waiting for transfers between devices, exchange(): return lax.all_to_all(pieces, axes, split_axis=0, concat_axis=0, tiled=True)  22.1 us
    dot_general x13, matrix products, dot(): lax.dot_general(a, b, (((ca,), (cb,)), ((), ())), preferred_element_type=...  10 us
    all_to_all x2, starting transfers between devices, exchange(): return lax.all_to_all(pieces, axes, split_axis=0, concat_axis=0, tiled=True)  8.52 us
    another operation x1, other arithmetic, on_device(): jnp.stack([out.reshape(8, 8 * cap, d), back.reshape(8, 8 * cap, d)], axis=1)  3.71 us
  transfers between devices with their start and end apart: 3, of which 3 were waited for; matrix products, arithmetic and copies ran while one was open for 3% of the time, Pallas kernels for 0%

profile of v2, /device:TPU:6, one launch (start us, length us, event | category | flops | bytes accessed | tf_op | source)
XLA Modules:
  0.0 128.2 jit_solution(10266414920841373095)
XLA Ops:
  0.7 1.2 convolution_convert_fusion.6
  1.8 1.1 fusion.4
  3.0 17.4 %all_to_all.30 = bf16[8,12,768]{2,1,0:T(8,128)(2,1)S(1)} all-to-all(bf16[8,12,768]{2,1,0:T(8,128)(2,1)S(1)} %broadcast_in_dim.14), channel_id=1, replica_groups=mesh['zl'=2,'y'=8,'x'=4,'zh'=4,'c'=2] {'y'}, dimensions={0} | all-to-all | bytes 294912 | tf_op jit(solution)/shard_map/all_to_all | solution.py:16
  20.7 19.6 %all_to_all.31 = bf16[8,2,48,768]{3,2,1,0:T(8,128)(2,1)S(1)} all-to-all(bf16[8,2,48,768]{3,2,1,0:T(8,128)(2,1)S(1)} %broadcast_in_dim.31), channel_id=1, replica_groups=mesh['zl'=2,'y'=8,'x'=4,'zh'=4,'c'=2] {'zl','x'}, dimensions={0} | all-to-all | bytes 2359296 | tf_op jit(solution)/shard_map/all_to_all | solution.py:16
  40.4 0.9 copy-done.2
  42.7 1.9 %collective-permute-start = (f32[3,128,384]{2,1,0:T(8,128)S(1)}, f32[3,128,384]{2,1,0:T(8,128)S(1)}, u32[]{:S(2)}, u32[]{:S(2)}) collective-permute-start(f32[3,128,384]{2,1,0:T(8,128)S(1)} %constant_dynamic-slice_fusion), channel_id=1, source_target_pairs={{0,1},{1,0},{2,3},{3,2},{4,5},{5,4},{6,7},{7,6},{8,9},{9,8},{10,11... | collective-permute-start | bytes 1769480 | tf_op jit(solution)/shard_map/ppermute | solution.py:56
  44.6 2.0 %collective-permute-done = f32[3,128,384]{2,1,0:T(8,128)S(1)} collective-permute-done((f32[3,128,384]{2,1,0:T(8,128)S(1)}, f32[3,128,384]{2,1,0:T(8,128)S(1)}, u32[]{:S(2)}, u32[]{:S(2)}) %collective-permute-start) | collective-permute-done | bytes 589856 | tf_op jit(solution)/shard_map/ppermute | solution.py:56
  46.7 21.4 %all_to_all.32 = bf16[4,3,32,384]{3,2,1,0:T(8,128)(2,1)S(1)} all-to-all(bf16[4,3,32,384]{3,2,1,0:T(8,128)(2,1)S(1)} %bitcast.114), channel_id=1, replica_groups=mesh['zl'=2,'y'=8,'x'=4,'zh'=4,'c'=2] {'zh'}, dimensions={0} | all-to-all | bytes 589824 | tf_op jit(solution)/shard_map/all_to_all | solution.py:16
  68.2 13.2 %all_to_all.33 = bf16[4,3,32,384]{3,2,1,0:T(8,128)(2,1)S(1)} all-to-all(bf16[4,3,32,384]{3,2,1,0:T(8,128)(2,1)S(1)} %broadcast_in_dim.32), channel_id=1, replica_groups=mesh['zl'=2,'y'=8,'x'=4,'zh'=4,'c'=2] {'zh'}, dimensions={0} | all-to-all | bytes 589824 | tf_op jit(solution)/shard_map/all_to_all | solution.py:16
  81.5 2.2 %all_gather.3 = bf16[8,3,32,384]{3,2,1,0:T(8,128)(2,1)S(1)} all-gather(bf16[4,3,32,384]{3,2,1,0:T(8,128)(2,1)S(1)} %all_to_all.33), channel_id=1, replica_groups=mesh['zl'=2,'y'=8,'x'=4,'zh'=4,'c'=2] {'c'}, dimensions={0}, use_global_device_ids=true | all-gather | bytes 884736 | tf_op jit(solution)/shard_map/all_gather | solution.py:71
  84.1 1.1 copy.26
  85.9 1.1 copy.27
  87.0 3.7 %pad_maximum_fusion.1 = bf16[8,2,48,768]{3,1,2,0:T(2,128)(2,1)} fusion(bf16[8,1,48,768]{3,1,2,0:T(2,128)(2,1)S(1)} %copy.27, bf16[8,1,48,768]{3,1,2,0:T(2,128)(2,1)S(1)} %copy.26), kind=kLoop, calls=%fused_computation.13 | loop fusion | flops 2359296 | bytes 2359296 | tf_op jit(solution)/shard_map/stack | solution.py:76
  90.7 5.1 %all-to-all-start.4 = ((bf16[8,2,48,768]{3,1,2,0:T(2,128)(2,1)}), bf16[8,2,48,768]{3,1,2,0:T(2,128)(2,1)S(1)}, u32[]{:S(2)}, u32[]{:S(2)}) async-start(bf16[8,2,48,768]{3,1,2,0:T(2,128)(2,1)} %pad_maximum_fusion.1), calls=%async_computation.4 | async-start | bytes 2359296 | tf_op jit(solution)/shard_map/all_to_all | solution.py:16
  95.8 1.1 fusion.2
  97.0 14.3 %all-to-all-done.4 = bf16[8,2,48,768]{3,1,2,0:T(2,128)(2,1)S(1)} async-done(((bf16[8,2,48,768]{3,1,2,0:T(2,128)(2,1)}), bf16[8,2,48,768]{3,1,2,0:T(2,128)(2,1)S(1)}, u32[]{:S(2)}, u32[]{:S(2)}) %all-to-all-start.4) | async-done | bytes 1179680 | tf_op jit(solution)/shard_map/all_to_all | solution.py:16
  111.3 0.6 add_convert_fusion.1
  111.9 0.7 copy.29
  112.6 3.4 %all-to-all-start.5 = ((bf16[8,12,768]{2,1,0:T(8,128)(2,1)}), bf16[8,12,768]{2,1,0:T(8,128)(2,1)S(1)}, u32[]{:S(2)}, u32[]{:S(2)}) async-start(bf16[8,12,768]{2,1,0:T(8,128)(2,1)} %copy.29), calls=%async_computation.5 | async-start | bytes 393216 | tf_op jit(solution)/shard_map/all_to_all | solution.py:16
  116.0 1.1 fusion.3
  117.1 1.2 fusion.1
  118.3 7.8 %all-to-all-done.5 = bf16[8,12,768]{2,1,0:T(8,128)(2,1)S(1)} async-done(((bf16[8,12,768]{2,1,0:T(8,128)(2,1)}), bf16[8,12,768]{2,1,0:T(8,128)(2,1)S(1)}, u32[]{:S(2)}, u32[]{:S(2)}) %all-to-all-start.5) | async-done | bytes 147488 | tf_op jit(solution)/shard_map/all_to_all | solution.py:16
  126.2 1.0 convolution_convert_fusion.5
  127.2 1.0 convolution_convert_fusion.4
  (33 shorter events, 3.2 us)
Async XLA Ops:
  0.6 41.5 %copy-start = (bf16[1,256,768]{2,1,0:T(8,128)(2,1)S(1)}, bf16[1,256,768]{2,1,0:T(8,128)(2,1)}, u32[]{:S(2)}) copy-start(bf16[1,256,768]{2,1,0:T(8,128)(2,1)} %param.11) | copy-start | bytes 1179652
  40.3 1.0 copy-start.2
  40.4 1.3 %copy-start.1 = (bf16[1,768,256]{2,1,0:T(8,128)(2,1)S(1)}, bf16[1,768,256]{2,1,0:T(8,128)(2,1)}, u32[]{:S(2)}) copy-start(bf16[1,768,256]{2,1,0:T(8,128)(2,1)} %param.9) | copy-start | bytes 1179652
  42.7 3.9 %collective-permute-start = (f32[3,128,384]{2,1,0:T(8,128)S(1)}, f32[3,128,384]{2,1,0:T(8,128)S(1)}, u32[]{:S(2)}, u32[]{:S(2)}) collective-permute-start(f32[3,128,384]{2,1,0:T(8,128)S(1)} %constant_dynamic-slice_fusion), channel_id=1, source_target_pairs={{0,1},{1,0},{2,3},{3,2},{4,5},{5,4},{6,7},{7,6},{8,9},{9,8},{10,11... | collective-permute-start | bytes 1769480 | tf_op jit(solution)/shard_map/ppermute | solution.py:56
  90.7 20.5 %all-to-all-start.4 = ((bf16[8,2,48,768]{3,1,2,0:T(2,128)(2,1)}), bf16[8,2,48,768]{3,1,2,0:T(2,128)(2,1)S(1)}, u32[]{:S(2)}, u32[]{:S(2)}) async-start(bf16[8,2,48,768]{3,1,2,0:T(2,128)(2,1)} %pad_maximum_fusion.1), calls=%async_computation.4 | async-start | bytes 2359296 | tf_op jit(solution)/shard_map/all_to_all | solution.py:16
  112.6 13.5 %all-to-all-start.5 = ((bf16[8,12,768]{2,1,0:T(8,128)(2,1)}), bf16[8,12,768]{2,1,0:T(8,128)(2,1)S(1)}, u32[]{:S(2)}, u32[]{:S(2)}) async-start(bf16[8,12,768]{2,1,0:T(8,128)(2,1)} %copy.29), calls=%async_computation.5 | async-start | bytes 393216 | tf_op jit(solution)/shard_map/all_to_all | solution.py:16
  116.0 10.1 %copy-start.3 = (s32[1,1,6]{2,1,0:T(1,128)S(1)}, s32[1,1,6]{2,1,0:T(1,128)}, u32[]{:S(2)}) copy-start(s32[1,1,6]{2,1,0:T(1,128)} %param.12) | copy-start | bytes 76
  116.0 10.1 %copy-start.4 = (f32[1,1,6]{2,1,0:T(1,128)S(1)}, f32[1,1,6]{2,1,0:T(1,128)}, u32[]{:S(2)}) copy-start(f32[1,1,6]{2,1,0:T(1,128)} %param.13) | copy-start | bytes 76

commit v3 on v2

--- a/solution.py
+++ b/solution.py
@@ -1,6 +1,8 @@
 import jax
 import jax.numpy as jnp
 from jax import lax
+from jax.experimental import pallas as pl
+from jax.experimental.pallas import tpu as pltpu
 from jax.sharding import Mesh
 from jax.sharding import PartitionSpec as P
 
@@ -31,21 +33,81 @@
     return lax.dot_general(a, b, (((ca,), (cb,)), ((), ())), preferred_element_type=F32)
 
 
+def one_hot(slots_ref, shape, slot_dim, first):
+    slot = lax.broadcasted_iota(jnp.int32, shape, slot_dim) - first
+    token = lax.broadcasted_iota(jnp.int32, shape, 1 - slot_dim)
+    wanted = jnp.full(shape, -1, jnp.int32)
+    for s in range(slots_ref.shape[0]):
+        wanted = jnp.where(slot == s, slots_ref[s], wanted)
+    return (token == wanted).astype(F32).astype(BF16)
+
+
+def by_slot(weights_ref, rows, first, other):
+    slot = lax.broadcasted_iota(jnp.int32, (rows, 1), 0) - first
+    out = jnp.full((rows, 1), other, F32)
+    for s in range(weights_ref.shape[0]):
+        out = jnp.where(slot == s, weights_ref[s], out)
+    return out
+
+
+def pick_body(slots_ref, weights_ref, tokens_ref, cotangent_ref, out_ref):
+    cap = slots_ref.shape[0]
+    copies, rows, _ = out_ref.shape
+    hot = one_hot(slots_ref, (rows, tokens_ref.shape[0]), 0, 0)
+    hot_d = one_hot(slots_ref, (rows, tokens_ref.shape[0]), 0, cap)
+    picked = dot(hot, tokens_ref[...], 1, 0)
+    d_rows = by_slot(weights_ref, rows, cap, 0.0) * dot(hot_d, cotangent_ref[...], 1, 0)
+    packed = (picked + d_rows).astype(BF16)
+    for j in range(copies):
+        out_ref[j] = packed
+
+
+def place_body(slots_ref, weights_ref, pieces_ref, mixed_ref, grad_ref):
+    cap = slots_ref.shape[0]
+    copies, rows, _ = pieces_ref.shape
+    tok = mixed_ref.shape[0]
+    acc = pieces_ref[0].astype(F32)
+    for j in range(1, copies):
+        acc = acc + pieces_ref[j].astype(F32)
+    acc = (acc * by_slot(weights_ref, rows, 0, 1.0)).astype(BF16)
+    mixed_ref[...] = dot(one_hot(slots_ref, (tok, rows), 1, 0), acc, 1, 0).astype(BF16)
+    grad_ref[...] = dot(one_hot(slots_ref, (tok, rows), 1, cap), acc, 1, 0).astype(BF16)
+
+
+SMEM = pl.BlockSpec(memory_space=pltpu.SMEM)
+VMEM = pl.BlockSpec(memory_space=pltpu.VMEM)
+
+
+def pick(slots, weights, tokens, cotangent, copies):
+    return pl.pallas_call(
+        pick_body,
+        in_specs=[SMEM, SMEM, VMEM, VMEM],
+        out_specs=VMEM,
+        out_shape=pltpu.VMEM((copies, 2 * slots.shape[0], tokens.shape[1]), BF16),
+    )(slots, weights, tokens, cotangent)
+
+
+def place(slots, weights, pieces, tok):
+    out = jax.ShapeDtypeStruct((tok, pieces.shape[2]), BF16)
+    return pl.pallas_call(
+        place_body, in_specs=[SMEM, SMEM, VMEM], out_specs=(VMEM, VMEM), out_shape=(out, out)
+    )(slots, weights, pltpu.with_memory_space_constraint(pieces, pltpu.VMEM))
+
+
 def on_device(tokens, cotangent, w_gate, w_up, w_down, slot_token, route_weight):
     w_gate, w_up, w_down = w_gate[0], w_up[0], w_down[0]
     slots, weights = slot_token[0, 0], route_weight[0, 0]
     tok, d = tokens.shape
     cap = slots.shape[0]
     ff = w_gate.shape[1]
-    one_hot = (slots[:, None] == jnp.arange(tok, dtype=jnp.int32)[None, :]).astype(BF16)
-    picked = dot(one_hot, tokens, 1, 0).astype(BF16)
-    d_rows = (weights[:, None] * dot(one_hot, cotangent, 1, 0)).astype(BF16)
 
     half = ff // 2
     kept_at = lax.axis_index("c").astype(jnp.uint32) * half
     sent_at = half - kept_at
-    near, kept_at, sent_at = lax.optimization_barrier((jnp.concatenate([picked, d_rows]), kept_at, sent_at))
-    near = spread(near, "y", 8)
+    near, kept_at, sent_at = lax.optimization_barrier(
+        (pick(slots, weights, tokens, cotangent, 8), kept_at, sent_at)
+    )
+    near = exchange(near, "y")
     near = near.reshape(8, 2, cap, d).transpose(1, 0, 2, 3).reshape(2, 8 * cap, d)
     rows = spread(near, ("zl", "x"), 8)
     n = 64 * cap
@@ -74,11 +136,9 @@
     out = dot(hidden, w_down, 0, 0).astype(BF16)
     back = (dot(d_gate, w_gate, 0, 1) + dot(d_up, w_up, 0, 1)).astype(BF16)
     both = jnp.stack([out.reshape(8, 8 * cap, d), back.reshape(8, 8 * cap, d)], axis=1)
-    both = total(exchange(both, ("zl", "x"))).astype(BF16)
+    both = lax.optimization_barrier(jnp.sum(exchange(both, ("zl", "x")).astype(F32), axis=0).astype(BF16))
     both = both.reshape(2, 8, cap, d).transpose(1, 0, 2, 3).reshape(8, 2 * cap, d)
-    both = total(exchange(both, "y"))
-    mixed = dot(one_hot, (weights[:, None] * both[:cap]).astype(BF16), 0, 0).astype(BF16)
-    grad_tokens = dot(one_hot, both[cap:].astype(BF16), 0, 0).astype(BF16)
+    mixed, grad_tokens = place(slots, weights, exchange(both, "y"), tok)
 
     grad_gate = dot(all_rows, d_gate, 0, 1).astype(BF16)
     grad_up = dot(all_rows, d_up, 0, 1).astype(BF16)

time: 129 us -> 123 us (0.953)
  matrix products: 10 us -> 5.72 us
  other arithmetic: 4.61 us -> 1.55 us
  Pallas kernels: 0 us -> 2.89 us
  local copies, waits for them, and re-layouts: 4.29 us -> 2.27 us
    dot_general x13 -> x9, matrix products: 10 us -> 5.72 us  [dot(): lax.dot_general(a, b, (((ca,), (cb,)), ((), ())), preferred_element_type=...]
    pallas_call x0 -> x2, Pallas kernels: none -> 2.89 us  [the longest x1 1.63 us: place(): pl.pallas_call(place_body, in_specs=[SMEM, SMEM, VMEM], out_specs=(VMEM,...]
    another operation x1, other arithmetic: 3.71 us -> 1.14 us  [on_device(): jnp.stack([out.reshape(8, 8 * cap, d), back.reshape(8, 8 * cap, d)], axis=1)]
    another operation x2 -> x0, local copies, waits for them, and re-layouts: 2.11 us -> none  [on_device(): jnp.stack([out.reshape(8, 8 * cap, d), back.reshape(8, 8 * cap, d)], axis=1)]
where the time goes in v3:
time: 123 us; the launch traced here: 122 us
  blocking collectives  73.8 us (60%)
  waiting for transfers between devices  24.1 us (20%)
  starting transfers between devices  10.4 us (8%)
  matrix products  5.72 us (5%)
  Pallas kernels  2.89 us (2%)
  local copies, waits for them, and re-layouts  2.27 us (2%)
  other arithmetic  1.55 us (1%)
    all_to_all x4, blocking collectives, exchange(): return lax.all_to_all(pieces, axes, split_axis=0, concat_axis=0, tiled=True)  71.6 us
    all_to_all x2, waiting for transfers between devices, exchange(): return lax.all_to_all(pieces, axes, split_axis=0, concat_axis=0, tiled=True)  22.1 us
    all_to_all x2, starting transfers between devices, exchange(): return lax.all_to_all(pieces, axes, split_axis=0, concat_axis=0, tiled=True)  8.51 us
    dot_general x9, matrix products, dot(): lax.dot_general(a, b, (((ca,), (cb,)), ((), ())), preferred_element_type=...  5.72 us
  transfers between devices with their start and end apart: 3, of which 3 were waited for; matrix products, arithmetic and copies ran while one was open for 3% of the time, Pallas kernels for 0%

profile of v3, /device:TPU:6, one launch (start us, length us, event | category | flops | bytes accessed | tf_op | source)
XLA Modules:
  0.0 121.6 jit_solution(12973419183616150594)
XLA Ops:
  0.7 1.3 %shard_map.110 = bf16[8,12,768]{2,1,0:T(8,128)(2,1)S(1)} custom-call(s32[6]{0:T(128)} %bitcast.112, f32[6]{0:T(128)} %bitcast.114, bf16[128,768]{1,0:T(8,128)(2,1)} %tokens_ref.1, bf16[128,768]{1,0:T(8,128)(2,1)} %cotangent_ref.1), custom_call_target="tpu_custom_call" | custom-call | tf_op jit(solution)/shard_map/pallas_call | solution.py:82
  1.9 17.4 %all_to_all.30 = bf16[8,12,768]{2,1,0:T(8,128)(2,1)S(1)} all-to-all(bf16[8,12,768]{2,1,0:T(8,128)(2,1)S(1)} %shard_map.110), channel_id=1, replica_groups=mesh['zl'=2,'y'=8,'x'=4,'zh'=4,'c'=2] {'y'}, dimensions={0} | all-to-all | bytes 294912 | tf_op jit(solution)/shard_map/all_to_all | solution.py:18
  19.6 19.6 %all_to_all.31 = bf16[8,2,48,768]{3,2,1,0:T(8,128)(2,1)S(1)} all-to-all(bf16[8,2,48,768]{3,2,1,0:T(8,128)(2,1)S(1)} %broadcast_in_dim.23), channel_id=1, replica_groups=mesh['zl'=2,'y'=8,'x'=4,'zh'=4,'c'=2] {'zl','x'}, dimensions={0} | all-to-all | bytes 2359296 | tf_op jit(solution)/shard_map/all_to_all | solution.py:18
  39.3 0.9 copy-done.2
  40.2 0.4 convolution_bitcast_fusion.1
  40.6 0.4 convolution_bitcast_fusion.2
  41.1 0.4 convolution_bitcast_fusion
  41.6 1.9 %collective-permute-start = (f32[3,128,384]{2,1,0:T(8,128)S(1)}, f32[3,128,384]{2,1,0:T(8,128)S(1)}, u32[]{:S(2)}, u32[]{:S(2)}) collective-permute-start(f32[3,128,384]{2,1,0:T(8,128)S(1)} %constant_dynamic-slice_fusion), channel_id=1, source_target_pairs={{0,1},{1,0},{2,3},{3,2},{4,5},{5,4},{6,7},{7,6},{8,9},{9,8},{10,11... | collective-permute-start | bytes 1769480 | tf_op jit(solution)/shard_map/ppermute | solution.py:118
  43.5 2.0 %collective-permute-done = f32[3,128,384]{2,1,0:T(8,128)S(1)} collective-permute-done((f32[3,128,384]{2,1,0:T(8,128)S(1)}, f32[3,128,384]{2,1,0:T(8,128)S(1)}, u32[]{:S(2)}, u32[]{:S(2)}) %collective-permute-start) | collective-permute-done | bytes 589856 | tf_op jit(solution)/shard_map/ppermute | solution.py:118
  45.6 21.3 %all_to_all.32 = bf16[4,3,32,384]{3,2,1,0:T(8,128)(2,1)S(1)} all-to-all(bf16[4,3,32,384]{3,2,1,0:T(8,128)(2,1)S(1)} %bitcast.106), channel_id=1, replica_groups=mesh['zl'=2,'y'=8,'x'=4,'zh'=4,'c'=2] {'zh'}, dimensions={0} | all-to-all | bytes 589824 | tf_op jit(solution)/shard_map/all_to_all | solution.py:18
  67.1 13.3 %all_to_all.33 = bf16[4,3,32,384]{3,2,1,0:T(8,128)(2,1)S(1)} all-to-all(bf16[4,3,32,384]{3,2,1,0:T(8,128)(2,1)S(1)} %broadcast_in_dim.24), channel_id=1, replica_groups=mesh['zl'=2,'y'=8,'x'=4,'zh'=4,'c'=2] {'zh'}, dimensions={0} | all-to-all | bytes 589824 | tf_op jit(solution)/shard_map/all_to_all | solution.py:18
  80.4 2.2 %all_gather.3 = bf16[8,3,32,384]{3,2,1,0:T(8,128)(2,1)S(1)} all-gather(bf16[4,3,32,384]{3,2,1,0:T(8,128)(2,1)S(1)} %all_to_all.33), channel_id=1, replica_groups=mesh['zl'=2,'y'=8,'x'=4,'zh'=4,'c'=2] {'c'}, dimensions={0}, use_global_device_ids=true | all-gather | bytes 884736 | tf_op jit(solution)/shard_map/all_gather | solution.py:133
  83.0 0.4 fusion.8
  83.4 0.4 fusion
  83.8 1.1 pad_maximum_fusion.1
  84.9 5.1 %all-to-all-start.4 = ((bf16[8,2,48,768]{3,2,1,0:T(8,128)(2,1)}), bf16[8,2,48,768]{3,2,1,0:T(8,128)(2,1)S(1)}, u32[]{:S(2)}, u32[]{:S(2)}) async-start(bf16[8,2,48,768]{3,2,1,0:T(8,128)(2,1)} %pad_maximum_fusion.1), calls=%async_computation.4 | async-start | bytes 2359296 | tf_op jit(solution)/shard_map/all_to_all | solution.py:18
  90.0 1.2 fusion.2
  91.2 14.3 %all-to-all-done.4 = bf16[8,2,48,768]{3,2,1,0:T(8,128)(2,1)S(1)} async-done(((bf16[8,2,48,768]{3,2,1,0:T(8,128)(2,1)}), bf16[8,2,48,768]{3,2,1,0:T(8,128)(2,1)S(1)}, u32[]{:S(2)}, u32[]{:S(2)}) %all-to-all-start.4) | async-done | bytes 1179680 | tf_op jit(solution)/shard_map/all_to_all | solution.py:18
  105.8 0.7 copy.30
  106.5 3.4 %all-to-all-start.5 = ((bf16[8,12,768]{2,1,0:T(8,128)(2,1)}), bf16[8,12,768]{2,1,0:T(8,128)(2,1)S(1)}, u32[]{:S(2)}, u32[]{:S(2)}) async-start(bf16[8,12,768]{2,1,0:T(8,128)(2,1)} %copy.30), calls=%async_computation.5 | async-start | bytes 393216 | tf_op jit(solution)/shard_map/all_to_all | solution.py:18
  109.9 1.1 fusion.3
  111.0 1.2 fusion.1
  112.1 7.8 %all-to-all-done.5.pieces_ref = bf16[8,12,768]{2,1,0:T(8,128)(2,1)S(1)} async-done(((bf16[8,12,768]{2,1,0:T(8,128)(2,1)}), bf16[8,12,768]{2,1,0:T(8,128)(2,1)S(1)}, u32[]{:S(2)}, u32[]{:S(2)}) %all-to-all-start.5) | async-done | bytes 147488 | tf_op jit(solution)/shard_map/all_to_all | solution.py:18
  120.0 1.6 %shard_map.111 = (bf16[128,768]{1,0:T(8,128)(2,1)}, bf16[128,768]{1,0:T(8,128)(2,1)}) custom-call(s32[6]{0:T(128)} %bitcast.113, f32[6]{0:T(128)} %bitcast.115, bf16[8,12,768]{2,1,0:T(8,128)(2,1)S(1)} %all-to-all-done.5.pieces_ref), custom_call_target="tpu_custom_call" | custom-call | tf_op jit(solution)/shard_map/pallas_call | solution.py:92
  (23 shorter events, 1.4 us)
Async XLA Ops:
  0.6 40.4 %copy-start = (bf16[1,256,768]{2,1,0:T(8,128)(2,1)S(1)}, bf16[1,256,768]{2,1,0:T(8,128)(2,1)}, u32[]{:S(2)}) copy-start(bf16[1,256,768]{2,1,0:T(8,128)(2,1)} %param.11) | copy-start | bytes 1179652
  39.2 1.0 copy-start.2
  39.3 1.3 %copy-start.1 = (bf16[1,768,256]{2,1,0:T(8,128)(2,1)S(1)}, bf16[1,768,256]{2,1,0:T(8,128)(2,1)}, u32[]{:S(2)}) copy-start(bf16[1,768,256]{2,1,0:T(8,128)(2,1)} %param.9) | copy-start | bytes 1179652
  41.6 3.9 %collective-permute-start = (f32[3,128,384]{2,1,0:T(8,128)S(1)}, f32[3,128,384]{2,1,0:T(8,128)S(1)}, u32[]{:S(2)}, u32[]{:S(2)}) collective-permute-start(f32[3,128,384]{2,1,0:T(8,128)S(1)} %constant_dynamic-slice_fusion), channel_id=1, source_target_pairs={{0,1},{1,0},{2,3},{3,2},{4,5},{5,4},{6,7},{7,6},{8,9},{9,8},{10,11... | collective-permute-start | bytes 1769480 | tf_op jit(solution)/shard_map/ppermute | solution.py:118
  84.9 20.5 %all-to-all-start.4 = ((bf16[8,2,48,768]{3,2,1,0:T(8,128)(2,1)}), bf16[8,2,48,768]{3,2,1,0:T(8,128)(2,1)S(1)}, u32[]{:S(2)}, u32[]{:S(2)}) async-start(bf16[8,2,48,768]{3,2,1,0:T(8,128)(2,1)} %pad_maximum_fusion.1), calls=%async_computation.4 | async-start | bytes 2359296 | tf_op jit(solution)/shard_map/all_to_all | solution.py:18
  106.5 13.5 %all-to-all-start.5 = ((bf16[8,12,768]{2,1,0:T(8,128)(2,1)}), bf16[8,12,768]{2,1,0:T(8,128)(2,1)S(1)}, u32[]{:S(2)}, u32[]{:S(2)}) async-start(bf16[8,12,768]{2,1,0:T(8,128)(2,1)} %copy.30), calls=%async_computation.5 | async-start | bytes 393216 | tf_op jit(solution)/shard_map/all_to_all | solution.py:18

commit v4 on v3

--- a/solution.py
+++ b/solution.py
@@ -50,48 +50,97 @@
     return out
 
 
-def pick_body(slots_ref, weights_ref, tokens_ref, cotangent_ref, out_ref):
+def pick_body(slots_ref, weights_ref, *refs):
+    sources, (out_ref, *weight_refs, tokens_ref, cotangent_ref, sems) = refs[:4], refs[4:]
+    copies = [
+        pltpu.make_async_copy(src, dst, sems.at[i])
+        for i, (src, dst) in enumerate(zip(sources, (tokens_ref, cotangent_ref, *weight_refs)))
+    ]
+    for copy in copies:
+        copy.start()
     cap = slots_ref.shape[0]
-    copies, rows, _ = out_ref.shape
+    count, rows, _ = out_ref.shape
     hot = one_hot(slots_ref, (rows, tokens_ref.shape[0]), 0, 0)
     hot_d = one_hot(slots_ref, (rows, tokens_ref.shape[0]), 0, cap)
+    scale = by_slot(weights_ref, rows, cap, 0.0)
+    copies[0].wait()
+    copies[1].wait()
     picked = dot(hot, tokens_ref[...], 1, 0)
-    d_rows = by_slot(weights_ref, rows, cap, 0.0) * dot(hot_d, cotangent_ref[...], 1, 0)
-    packed = (picked + d_rows).astype(BF16)
-    for j in range(copies):
+    packed = (picked + scale * dot(hot_d, cotangent_ref[...], 1, 0)).astype(BF16)
+    for j in range(count):
         out_ref[j] = packed
-
-
-def place_body(slots_ref, weights_ref, pieces_ref, mixed_ref, grad_ref):
-    cap = slots_ref.shape[0]
-    copies, rows, _ = pieces_ref.shape
+    for copy in copies[2:]:
+        copy.wait()
+
+
+def place_body(hot_ref, scale_ref, pieces_ref, mixed_ref, grad_ref):
     tok = mixed_ref.shape[0]
     acc = pieces_ref[0].astype(F32)
-    for j in range(1, copies):
+    for j in range(1, pieces_ref.shape[0]):
         acc = acc + pieces_ref[j].astype(F32)
-    acc = (acc * by_slot(weights_ref, rows, 0, 1.0)).astype(BF16)
-    mixed_ref[...] = dot(one_hot(slots_ref, (tok, rows), 1, 0), acc, 1, 0).astype(BF16)
-    grad_ref[...] = dot(one_hot(slots_ref, (tok, rows), 1, cap), acc, 1, 0).astype(BF16)
+    acc = (acc * scale_ref[:, :1]).astype(BF16)
+    mixed_ref[...] = dot(hot_ref[:tok], acc, 1, 0).astype(BF16)
+    grad_ref[...] = dot(hot_ref[tok:], acc, 1, 0).astype(BF16)
+
+
+def regroup_body(pieces_ref, out_ref):
+    targets, rows, d = out_ref.shape
+    cap = rows // 2
+    padded = -(-rows // 8) * 8
+    acc = pieces_ref[0].astype(F32)
+    for j in range(1, pieces_ref.shape[0]):
+        acc = acc + pieces_ref[j].astype(F32)
+    acc = acc.reshape(targets * rows, d).astype(BF16)
+    shape = (targets * padded, targets * rows)
+    at = lax.broadcasted_iota(jnp.int32, shape, 0)
+    target, row = at // padded, at % padded
+    source = jnp.where(row < cap, target * cap + row, (targets - 1 + target) * cap + row)
+    source = jnp.where(row < rows, source, -1)
+    move = (lax.broadcasted_iota(jnp.int32, shape, 1) == source).astype(F32).astype(BF16)
+    out_ref[...] = dot(move, acc, 1, 0).astype(BF16).reshape(targets, padded, d)[:, :rows]
 
 
 SMEM = pl.BlockSpec(memory_space=pltpu.SMEM)
 VMEM = pl.BlockSpec(memory_space=pltpu.VMEM)
-
-
-def pick(slots, weights, tokens, cotangent, copies):
+ANY = pl.BlockSpec(memory_space=pl.ANY)
+
+
+def pick(slots, weights, tokens, cotangent, matrices, copies):
     return pl.pallas_call(
         pick_body,
-        in_specs=[SMEM, SMEM, VMEM, VMEM],
-        out_specs=VMEM,
-        out_shape=pltpu.VMEM((copies, 2 * slots.shape[0], tokens.shape[1]), BF16),
-    )(slots, weights, tokens, cotangent)
-
-
-def place(slots, weights, pieces, tok):
-    out = jax.ShapeDtypeStruct((tok, pieces.shape[2]), BF16)
+        in_specs=[SMEM, SMEM, ANY, ANY, ANY, ANY],
+        out_specs=(VMEM, VMEM, VMEM),
+        out_shape=(
+            pltpu.VMEM((copies, 2 * slots.shape[0], tokens.shape[1]), BF16),
+            *(pltpu.VMEM(w.shape, BF16) for w in matrices),
+        ),
+        scratch_shapes=[
+            pltpu.VMEM(tokens.shape, BF16),
+            pltpu.VMEM(cotangent.shape, BF16),
+            pltpu.SemaphoreType.DMA((4,)),
+        ],
+    )(slots, weights, tokens, cotangent, *matrices)
+
+
+def on_chip(body, shape, dtype, *arrays):
     return pl.pallas_call(
-        place_body, in_specs=[SMEM, SMEM, VMEM], out_specs=(VMEM, VMEM), out_shape=(out, out)
-    )(slots, weights, pltpu.with_memory_space_constraint(pieces, pltpu.VMEM))
+        body, in_specs=[VMEM] * len(arrays), out_specs=VMEM, out_shape=pltpu.VMEM(shape, dtype)
+    )(*(pltpu.with_memory_space_constraint(x, pltpu.VMEM) for x in arrays))
+
+
+def spots(slots, weights, tok):
+    cap = slots.shape[0]
+    spot = jnp.concatenate([slots, jnp.where(slots >= 0, slots + tok, -1)])
+    hot = (jnp.arange(2 * tok, dtype=jnp.int32)[:, None] == spot[None, :]).astype(BF16)
+    scale = jnp.concatenate([weights, jnp.ones((cap,), F32)])
+    return hot, jnp.broadcast_to(scale[:, None], (2 * cap, 128))
+
+
+def place(hot, scale, pieces):
+    out = jax.ShapeDtypeStruct((hot.shape[0] // 2, pieces.shape[2]), BF16)
+    return pl.pallas_call(place_body, in_specs=[VMEM, VMEM, VMEM], out_specs=(VMEM, VMEM), out_shape=(out, out))(
+        *(pltpu.with_memory_space_constraint(x, pltpu.VMEM) for x in (hot, scale, pieces))
+    )
 
 
 def on_device(tokens, cotangent, w_gate, w_up, w_down, slot_token, route_weight):
@@ -104,20 +153,17 @@
     half = ff // 2
     kept_at = lax.axis_index("c").astype(jnp.uint32) * half
     sent_at = half - kept_at
-    near, kept_at, sent_at = lax.optimization_barrier(
-        (pick(slots, weights, tokens, cotangent, 8), kept_at, sent_at)
+    (near, w_gate, w_up), kept_at, sent_at = lax.optimization_barrier(
+        (pick(slots, weights, tokens, cotangent, (w_gate, w_up), 8), kept_at, sent_at)
     )
     near = exchange(near, "y")
     near = near.reshape(8, 2, cap, d).transpose(1, 0, 2, 3).reshape(2, 8 * cap, d)
     rows = spread(near, ("zl", "x"), 8)
     n = 64 * cap
-    all_rows = rows[:, 0].reshape(n, d)
-    all_grads = rows[:, 1].reshape(n, d)
-
+
+    all_rows, all_grads = (rows[:, i].reshape(n, d) for i in range(2))
     part = jnp.stack([dot(w_gate, all_rows, 0, 1), dot(w_up, all_rows, 0, 1), dot(w_down, all_grads, 1, 1)])
-    sent = lax.ppermute(
-        lax.dynamic_slice_in_dim(part, sent_at, half, axis=1), "c", [(0, 1), (1, 0)]
-    )
+    sent = lax.ppermute(lax.dynamic_slice_in_dim(part, sent_at, half, axis=1), "c", [(0, 1), (1, 0)])
     part = (lax.dynamic_slice_in_dim(part, kept_at, half, axis=1) + sent).astype(BF16)
     part = part.reshape(3, 4, ff // 8, n).transpose(1, 0, 2, 3)
     gate_sum, up_sum, hidden_grad = total(exchange(part, "zh"))
@@ -131,18 +177,22 @@
         ]
     ).astype(BF16)
     full = lax.all_gather(spread(own, "zh", 4), "c", axis=0, tiled=True)
+
     hidden, d_gate, d_up = (full[:, i].reshape(ff, n) for i in range(3))
-
     out = dot(hidden, w_down, 0, 0).astype(BF16)
     back = (dot(d_gate, w_gate, 0, 1) + dot(d_up, w_up, 0, 1)).astype(BF16)
     both = jnp.stack([out.reshape(8, 8 * cap, d), back.reshape(8, 8 * cap, d)], axis=1)
-    both = lax.optimization_barrier(jnp.sum(exchange(both, ("zl", "x")).astype(F32), axis=0).astype(BF16))
-    both = both.reshape(2, 8, cap, d).transpose(1, 0, 2, 3).reshape(8, 2 * cap, d)
-    mixed, grad_tokens = place(slots, weights, exchange(both, "y"), tok)
+    both, slots, weights = lax.optimization_barrier((both, slots, weights))
+    both = exchange(both, ("zl", "x"))
 
     grad_gate = dot(all_rows, d_gate, 0, 1).astype(BF16)
     grad_up = dot(all_rows, d_up, 0, 1).astype(BF16)
     grad_down = dot(hidden, all_grads, 1, 0).astype(BF16)
+    both, grad_gate, grad_up, grad_down, (hot, scale) = lax.optimization_barrier(
+        (both, grad_gate, grad_up, grad_down, spots(slots, weights, tok))
+    )
+    both = on_chip(regroup_body, (8, 2 * cap, d), BF16, both)
+    mixed, grad_tokens = place(hot, scale, exchange(both, "y"))
     return mixed, grad_tokens, grad_gate[None], grad_up[None], grad_down[None]
 
 

time: 123 us -> 121 us (0.984)
  blocking collectives: 73.8 us -> 86.8 us
  waiting for transfers between devices: 24.1 us -> 13.8 us
  starting transfers between devices: 10.4 us -> 7.17 us
  local copies, waits for them, and re-layouts: 2.27 us -> 0.61 us
    all_to_all x4 -> x5, blocking collectives: 71.6 us -> 84.6 us  [exchange(): return lax.all_to_all(pieces, axes, split_axis=0, concat_axis=0, tiled=True)]
    all_to_all x2 -> x1, waiting for transfers between devices: 22.1 us -> 11.9 us  [exchange(): return lax.all_to_all(pieces, axes, split_axis=0, concat_axis=0, tiled=True)]
    all_to_all x2 -> x1, starting transfers between devices: 8.51 us -> 5.25 us  [exchange(): return lax.all_to_all(pieces, axes, split_axis=0, concat_axis=0, tiled=True)]
    pallas_call x2 -> x3, Pallas kernels: 2.89 us -> 3.5 us  [the longest x1 2.15 us: pick(): pl.pallas_call(pick_body, in_specs=[SMEM, SMEM, ANY, ANY, ANY, ANY], out_...]
  transfers between devices with their start and end apart: 3 -> 2, of which waited for: 3 -> 2; matrix products, arithmetic and copies ran while one was open for 3% -> 3% of each run, Pallas kernels for 0% -> 0%
where the time goes in v4:
time: 121 us; the launch traced here: 120 us
  blocking collectives  86.8 us (72%)
  waiting for transfers between devices  13.8 us (11%)
  starting transfers between devices  7.17 us (6%)
  matrix products  5.71 us (5%)
  Pallas kernels  3.5 us (3%)
  other arithmetic  1.49 us (1%)
    all_to_all x5, blocking collectives, exchange(): return lax.all_to_all(pieces, axes, split_axis=0, concat_axis=0, tiled=True)  84.6 us
    all_to_all x1, waiting for transfers between devices, exchange(): return lax.all_to_all(pieces, axes, split_axis=0, concat_axis=0, tiled=True)  11.9 us
    dot_general x9, matrix products, dot(): lax.dot_general(a, b, (((ca,), (cb,)), ((), ())), preferred_element_type=...  5.71 us
    all_to_all x1, starting transfers between devices, exchange(): return lax.all_to_all(pieces, axes, split_axis=0, concat_axis=0, tiled=True)  5.25 us
  transfers between devices with their start and end apart: 2, of which 2 were waited for; matrix products, arithmetic and copies ran while one was open for 3% of the time, Pallas kernels for 0%

profile of v4, /device:TPU:6, one launch (start us, length us, event | category | flops | bytes accessed | tf_op | source)
XLA Modules:
  0.0 120.0 jit_solution(7600821304817757405)
XLA Ops:
  0.7 2.2 %shard_map.110 = (bf16[8,12,768]{2,1,0:T(8,128)(2,1)S(1)}, bf16[768,256]{1,0:T(8,128)(2,1)S(1)}, bf16[768,256]{1,0:T(8,128)(2,1)S(1)}) custom-call(s32[6]{0:T(128)} %bitcast.98, f32[6]{0:T(128)} %bitcast.96, bf16[128,768]{1,0:T(8,128)(2,1)} %refs_0_.1, bf16[128,768]{1,0:T(8,128)(2,1)} %refs_1_.1, bf16[768,256]{1,0:T(8,128)(2,1)} %bitcast.91, ...), custom_call_target="tpu_custom_call" | custom-call | tf_op jit(solution)/shard_map/pallas_call | solution.py:109
  2.8 17.4 %all_to_all.30 = bf16[8,12,768]{2,1,0:T(8,128)(2,1)S(1)} all-to-all(bf16[8,12,768]{2,1,0:T(8,128)(2,1)S(1)} %get-tuple-element.28), channel_id=1, replica_groups=mesh['zl'=2,'y'=8,'x'=4,'zh'=4,'c'=2] {'y'}, dimensions={0} | all-to-all | bytes 294912 | tf_op jit(solution)/shard_map/all_to_all | solution.py:18
  20.2 0.1 copy.20
  20.5 19.6 %all_to_all.31 = bf16[8,2,48,768]{3,2,1,0:T(8,128)(2,1)S(1)} all-to-all(bf16[8,2,48,768]{3,2,1,0:T(8,128)(2,1)S(1)} %broadcast_in_dim.35), channel_id=1, replica_groups=mesh['zl'=2,'y'=8,'x'=4,'zh'=4,'c'=2] {'zl','x'}, dimensions={0} | all-to-all | bytes 2359296 | tf_op jit(solution)/shard_map/all_to_all | solution.py:18
  40.2 0.4 convolution_bitcast_fusion.1
  40.6 0.4 convolution_bitcast_fusion.2
  41.1 0.4 convolution_bitcast_fusion
  41.6 1.9 %collective-permute-start = (f32[3,128,384]{2,1,0:T(8,128)S(1)}, f32[3,128,384]{2,1,0:T(8,128)S(1)}, u32[]{:S(2)}, u32[]{:S(2)}) collective-permute-start(f32[3,128,384]{2,1,0:T(8,128)S(1)} %constant_dynamic-slice_fusion), channel_id=1, source_target_pairs={{0,1},{1,0},{2,3},{3,2},{4,5},{5,4},{6,7},{7,6},{8,9},{9,8},{10,11... | collective-permute-start | bytes 1769480 | tf_op jit(solution)/shard_map/ppermute | solution.py:166
  43.5 2.0 %collective-permute-done = f32[3,128,384]{2,1,0:T(8,128)S(1)} collective-permute-done((f32[3,128,384]{2,1,0:T(8,128)S(1)}, f32[3,128,384]{2,1,0:T(8,128)S(1)}, u32[]{:S(2)}, u32[]{:S(2)}) %collective-permute-start) | collective-permute-done | bytes 589856 | tf_op jit(solution)/shard_map/ppermute | solution.py:166
  45.6 21.3 %all_to_all.32 = bf16[4,3,32,384]{3,2,1,0:T(8,128)(2,1)S(1)} all-to-all(bf16[4,3,32,384]{3,2,1,0:T(8,128)(2,1)S(1)} %bitcast.87), channel_id=1, replica_groups=mesh['zl'=2,'y'=8,'x'=4,'zh'=4,'c'=2] {'zh'}, dimensions={0} | all-to-all | bytes 589824 | tf_op jit(solution)/shard_map/all_to_all | solution.py:18
  67.1 13.3 %all_to_all.33 = bf16[4,3,32,384]{3,2,1,0:T(8,128)(2,1)S(1)} all-to-all(bf16[4,3,32,384]{3,2,1,0:T(8,128)(2,1)S(1)} %broadcast_in_dim.36), channel_id=1, replica_groups=mesh['zl'=2,'y'=8,'x'=4,'zh'=4,'c'=2] {'zh'}, dimensions={0} | all-to-all | bytes 589824 | tf_op jit(solution)/shard_map/all_to_all | solution.py:18
  80.4 2.2 %all_gather.3 = bf16[8,3,32,384]{3,2,1,0:T(8,128)(2,1)S(1)} all-gather(bf16[4,3,32,384]{3,2,1,0:T(8,128)(2,1)S(1)} %all_to_all.33), channel_id=1, replica_groups=mesh['zl'=2,'y'=8,'x'=4,'zh'=4,'c'=2] {'c'}, dimensions={0}, use_global_device_ids=true | all-gather | bytes 884736 | tf_op jit(solution)/shard_map/all_gather | solution.py:179
  82.7 0.4 convolution_convert_fusion
  83.0 0.4 fusion.7
  83.4 0.4 fusion
  83.8 1.1 pad_maximum_fusion.1
  84.9 5.2 %all-to-all-start.4 = ((bf16[8,2,48,768]{3,2,1,0:T(8,128)(2,1)}), bf16[8,2,48,768]{3,2,1,0:T(8,128)(2,1)S(1)}, u32[]{:S(2)}, u32[]{:S(2)}) async-start(bf16[8,2,48,768]{3,2,1,0:T(8,128)(2,1)} %pad_maximum_fusion.1), calls=%async_computation.4 | async-start | bytes 2359296 | tf_op jit(solution)/shard_map/all_to_all | solution.py:18
  90.3 1.1 convolution_convert_fusion.1
  91.4 1.1 convolution_convert_fusion.2
  92.6 1.2 convolution_convert_fusion.3
  93.7 11.9 %all-to-all-done.4.pieces_ref = bf16[8,2,48,768]{3,2,1,0:T(8,128)(2,1)S(1)} async-done(((bf16[8,2,48,768]{3,2,1,0:T(8,128)(2,1)}), bf16[8,2,48,768]{3,2,1,0:T(8,128)(2,1)S(1)}, u32[]{:S(2)}, u32[]{:S(2)}) %all-to-all-start.4) | async-done | bytes 1179680 | tf_op jit(solution)/shard_map/all_to_all | solution.py:18
  105.7 0.3 shard_map.111
  106.0 13.0 %all_to_all.34.pieces_ref = bf16[8,12,768]{2,1,0:T(8,128)(2,1)S(1)} all-to-all(bf16[8,12,768]{2,1,0:T(8,128)(2,1)S(1)} %shard_map.111), channel_id=1, replica_groups=mesh['zl'=2,'y'=8,'x'=4,'zh'=4,'c'=2] {'y'}, dimensions={0} | all-to-all | bytes 294912 | tf_op jit(solution)/shard_map/all_to_all | solution.py:18
  119.0 1.0 shard_map.112
  (28 shorter events, 0.8 us)
Async XLA Ops:
  0.6 40.4 %copy-start = (bf16[1,256,768]{2,1,0:T(8,128)(2,1)S(1)}, bf16[1,256,768]{2,1,0:T(8,128)(2,1)}, u32[]{:S(2)}) copy-start(bf16[1,256,768]{2,1,0:T(8,128)(2,1)} %param.11) | copy-start | bytes 1179652
  40.2 0.8 copy-start.1
  41.6 3.9 %collective-permute-start = (f32[3,128,384]{2,1,0:T(8,128)S(1)}, f32[3,128,384]{2,1,0:T(8,128)S(1)}, u32[]{:S(2)}, u32[]{:S(2)}) collective-permute-start(f32[3,128,384]{2,1,0:T(8,128)S(1)} %constant_dynamic-slice_fusion), channel_id=1, source_target_pairs={{0,1},{1,0},{2,3},{3,2},{4,5},{5,4},{6,7},{7,6},{8,9},{9,8},{10,11... | collective-permute-start | bytes 1769480 | tf_op jit(solution)/shard_map/ppermute | solution.py:166
  84.9 5.3 %copy-start.3 = (f32[1,1,6]{2,1,0:T(1,128)S(1)}, f32[1,1,6]{2,1,0:T(1,128)}, u32[]{:S(2)}) copy-start(f32[1,1,6]{2,1,0:T(1,128)} %param.13) | copy-start | bytes 76
  84.9 5.3 %copy-start.4 = (s32[1,1,6]{2,1,0:T(1,128)S(1)}, s32[1,1,6]{2,1,0:T(1,128)}, u32[]{:S(2)}) copy-start(s32[1,1,6]{2,1,0:T(1,128)} %param.12) | copy-start | bytes 76
  84.9 5.4 %copy-start.2 = (bf16[8,1,48,768]{3,2,1,0:T(8,128)(2,1)S(1)}, bf16[8,1,48,768]{3,2,1,0:T(8,128)(2,1)}, u32[]{:S(2)}) copy-start(bf16[8,1,48,768]{3,2,1,0:T(8,128)(2,1)} %copy-done.1) | copy-start | bytes 1769476
  84.9 20.7 %all-to-all-start.4 = ((bf16[8,2,48,768]{3,2,1,0:T(8,128)(2,1)}), bf16[8,2,48,768]{3,2,1,0:T(8,128)(2,1)S(1)}, u32[]{:S(2)}, u32[]{:S(2)}) async-start(bf16[8,2,48,768]{3,2,1,0:T(8,128)(2,1)} %pad_maximum_fusion.1), calls=%async_computation.4 | async-start | bytes 2359296 | tf_op jit(solution)/shard_map/all_to_all | solution.py:18

commit v5 on v4

--- a/solution.py
+++ b/solution.py
@@ -50,26 +50,26 @@
     return out
 
 
-def pick_body(slots_ref, weights_ref, *refs):
-    sources, (out_ref, *weight_refs, tokens_ref, cotangent_ref, sems) = refs[:4], refs[4:]
-    copies = [
-        pltpu.make_async_copy(src, dst, sems.at[i])
-        for i, (src, dst) in enumerate(zip(sources, (tokens_ref, cotangent_ref, *weight_refs)))
-    ]
+def pick_body(*refs):
+    sources, (out_ref, *matrix_refs, slots_ref, weights_ref, tokens_ref, cotangent_ref, sems) = refs[:6], refs[6:]
+    targets = (slots_ref, weights_ref, tokens_ref, cotangent_ref, *matrix_refs)
+    copies = [pltpu.make_async_copy(src, dst, sems.at[i]) for i, (src, dst) in enumerate(zip(sources, targets))]
     for copy in copies:
         copy.start()
+    copies[0].wait()
+    copies[1].wait()
     cap = slots_ref.shape[0]
     count, rows, _ = out_ref.shape
     hot = one_hot(slots_ref, (rows, tokens_ref.shape[0]), 0, 0)
     hot_d = one_hot(slots_ref, (rows, tokens_ref.shape[0]), 0, cap)
     scale = by_slot(weights_ref, rows, cap, 0.0)
-    copies[0].wait()
-    copies[1].wait()
+    copies[2].wait()
+    copies[3].wait()
     picked = dot(hot, tokens_ref[...], 1, 0)
     packed = (picked + scale * dot(hot_d, cotangent_ref[...], 1, 0)).astype(BF16)
     for j in range(count):
         out_ref[j] = packed
-    for copy in copies[2:]:
+    for copy in copies[4:]:
         copy.wait()
 
 
@@ -100,7 +100,6 @@
     out_ref[...] = dot(move, acc, 1, 0).astype(BF16).reshape(targets, padded, d)[:, :rows]
 
 
-SMEM = pl.BlockSpec(memory_space=pltpu.SMEM)
 VMEM = pl.BlockSpec(memory_space=pltpu.VMEM)
 ANY = pl.BlockSpec(memory_space=pl.ANY)
 
@@ -108,16 +107,18 @@
 def pick(slots, weights, tokens, cotangent, matrices, copies):
     return pl.pallas_call(
         pick_body,
-        in_specs=[SMEM, SMEM, ANY, ANY, ANY, ANY],
+        in_specs=[ANY] * 6,
         out_specs=(VMEM, VMEM, VMEM),
         out_shape=(
             pltpu.VMEM((copies, 2 * slots.shape[0], tokens.shape[1]), BF16),
             *(pltpu.VMEM(w.shape, BF16) for w in matrices),
         ),
         scratch_shapes=[
+            pltpu.SMEM(slots.shape, slots.dtype),
+            pltpu.SMEM(weights.shape, weights.dtype),
             pltpu.VMEM(tokens.shape, BF16),
             pltpu.VMEM(cotangent.shape, BF16),
-            pltpu.SemaphoreType.DMA((4,)),
+            pltpu.SemaphoreType.DMA((6,)),
         ],
     )(slots, weights, tokens, cotangent, *matrices)
 
@@ -151,10 +152,11 @@
     ff = w_gate.shape[1]
 
     half = ff // 2
-    kept_at = lax.axis_index("c").astype(jnp.uint32) * half
-    sent_at = half - kept_at
-    (near, w_gate, w_up), kept_at, sent_at = lax.optimization_barrier(
-        (pick(slots, weights, tokens, cotangent, (w_gate, w_up), 8), kept_at, sent_at)
+    other = 1 - lax.axis_index("c").astype(jnp.uint32)
+    sent_at = other * half
+    kept_at = half - sent_at
+    (near, w_gate, w_up), other, kept_at, sent_at = lax.optimization_barrier(
+        (pick(slots, weights, tokens, cotangent, (w_gate, w_up), 8), other, kept_at, sent_at)
     )
     near = exchange(near, "y")
     near = near.reshape(8, 2, cap, d).transpose(1, 0, 2, 3).reshape(2, 8 * cap, d)
@@ -163,8 +165,9 @@
 
     all_rows, all_grads = (rows[:, i].reshape(n, d) for i in range(2))
     part = jnp.stack([dot(w_gate, all_rows, 0, 1), dot(w_up, all_rows, 0, 1), dot(w_down, all_grads, 1, 1)])
-    sent = lax.ppermute(lax.dynamic_slice_in_dim(part, sent_at, half, axis=1), "c", [(0, 1), (1, 0)])
-    part = (lax.dynamic_slice_in_dim(part, kept_at, half, axis=1) + sent).astype(BF16)
+    sent = lax.all_gather(lax.dynamic_slice_in_dim(part, sent_at, half, axis=1).astype(BF16), "c")
+    sent = lax.dynamic_index_in_dim(sent, other, axis=0, keepdims=False)
+    part = (lax.dynamic_slice_in_dim(part, kept_at, half, axis=1) + sent.astype(F32)).astype(BF16)
     part = part.reshape(3, 4, ff // 8, n).transpose(1, 0, 2, 3)
     gate_sum, up_sum, hidden_grad = total(exchange(part, "zh"))
     sigmoid_gate = jax.nn.sigmoid(gate_sum)

time: 121 us -> 118 us (0.975)
  blocking collectives: 86.8 us -> 89 us
  waiting for transfers between devices: 13.8 us -> 11.8 us
  starting transfers between devices: 7.17 us -> 5.25 us
    all_gather x0 -> x1, blocking collectives: none -> 2.23 us  [on_device(): lax.all_gather(lax.dynamic_slice_in_dim(part, sent_at, half, axis=1).asty...]
    ppermute x1 -> x0, waiting for transfers between devices: 1.97 us -> none  [on_device(): lax.ppermute(lax.dynamic_slice_in_dim(part, sent_at, half, axis=1), 'c',...]
    ppermute x1 -> x0, starting transfers between devices: 1.92 us -> none  [on_device(): lax.ppermute(lax.dynamic_slice_in_dim(part, sent_at, half, axis=1), 'c',...]
  transfers between devices with their start and end apart: 2 -> 1, of which waited for: 2 -> 1; matrix products, arithmetic and copies ran while one was open for 3% -> 3% of each run, Pallas kernels for 0% -> 0%
where the time goes in v5:
time: 118 us
  blocking collectives  89 us (75%)
  waiting for transfers between devices  11.8 us (10%)
  matrix products  5.71 us (5%)
  starting transfers between devices  5.25 us (4%)
  Pallas kernels  2.75 us (2%)
  other arithmetic  1.51 us (1%)
    all_to_all x5, blocking collectives, exchange(): return lax.all_to_all(pieces, axes, split_axis=0, concat_axis=0, tiled=True)  84.6 us
    all_to_all x1, waiting for transfers between devices, exchange(): return lax.all_to_all(pieces, axes, split_axis=0, concat_axis=0, tiled=True)  11.8 us
    dot_general x9, matrix products, dot(): lax.dot_general(a, b, (((ca,), (cb,)), ((), ())), preferred_element_type=...  5.71 us
    all_to_all x1, starting transfers between devices, exchange(): return lax.all_to_all(pieces, axes, split_axis=0, concat_axis=0, tiled=True)  5.25 us
  transfers between devices with their start and end apart: 1, of which 1 were waited for; matrix products, arithmetic and copies ran while one was open for 3% of the time, Pallas kernels for 0%

profile of v5, /device:TPU:6, one launch (start us, length us, event | category | flops | bytes accessed | tf_op | source)
XLA Modules:
  0.0 117.6 jit_solution(577205579911466932)
XLA Ops:
  0.7 1.4 %shard_map.110 = (bf16[8,12,768]{2,1,0:T(8,128)(2,1)S(1)}, bf16[768,256]{1,0:T(8,128)(2,1)S(1)}, bf16[768,256]{1,0:T(8,128)(2,1)S(1)}) custom-call(s32[6]{0:T(128)} %bitcast.103, f32[6]{0:T(128)} %bitcast.101, bf16[128,768]{1,0:T(8,128)(2,1)} %refs_2_.1, bf16[128,768]{1,0:T(8,128)(2,1)} %refs_3_.1, bf16[768,256]{1,0:T(8,128)(2,1)} %bitcast.96, ...), custom_call_target="tpu_custom_call" | custom-call | tf_op jit(solution)/shard_map/pallas_call | solution.py:108
  2.1 17.4 %all_to_all.30 = bf16[8,12,768]{2,1,0:T(8,128)(2,1)S(1)} all-to-all(bf16[8,12,768]{2,1,0:T(8,128)(2,1)S(1)} %get-tuple-element.29), channel_id=1, replica_groups=mesh['zl'=2,'y'=8,'x'=4,'zh'=4,'c'=2] {'y'}, dimensions={0} | all-to-all | bytes 294912 | tf_op jit(solution)/shard_map/all_to_all | solution.py:18
  19.5 0.1 copy.20
  19.7 19.6 %all_to_all.31 = bf16[8,2,48,768]{3,2,1,0:T(8,128)(2,1)S(1)} all-to-all(bf16[8,2,48,768]{3,2,1,0:T(8,128)(2,1)S(1)} %broadcast_in_dim.35), channel_id=1, replica_groups=mesh['zl'=2,'y'=8,'x'=4,'zh'=4,'c'=2] {'zl','x'}, dimensions={0} | all-to-all | bytes 2359296 | tf_op jit(solution)/shard_map/all_to_all | solution.py:18
  39.5 0.4 convolution_bitcast_fusion.1
  39.9 0.4 convolution_bitcast_fusion.2
  40.3 0.4 convolution_bitcast_fusion
  40.9 2.2 %all-gather = bf16[6,128,384]{2,1,0:T(8,128)(2,1)S(1)} all-gather(bf16[3,128,384]{2,1,0:T(8,128)(2,1)S(1)} %dynamic-slice_convert_fusion), channel_id=2, replica_groups=mesh['zl'=2,'y'=8,'x'=4,'zh'=4,'c'=2] {'c'}, dimensions={0}, use_global_device_ids=true | all-gather | bytes 884736 | tf_op jit(solution)/shard_map/all_gather | solution.py:168
  43.1 0.1 fusion.1
  43.2 21.3 %all_to_all.32 = bf16[4,3,32,384]{3,2,1,0:T(8,128)(2,1)S(1)} all-to-all(bf16[4,3,32,384]{3,2,1,0:T(8,128)(2,1)S(1)} %bitcast.92), channel_id=1, replica_groups=mesh['zl'=2,'y'=8,'x'=4,'zh'=4,'c'=2] {'zh'}, dimensions={0} | all-to-all | bytes 589824 | tf_op jit(solution)/shard_map/all_to_all | solution.py:18
  64.7 13.3 %all_to_all.33 = bf16[4,3,32,384]{3,2,1,0:T(8,128)(2,1)S(1)} all-to-all(bf16[4,3,32,384]{3,2,1,0:T(8,128)(2,1)S(1)} %broadcast_in_dim.36), channel_id=1, replica_groups=mesh['zl'=2,'y'=8,'x'=4,'zh'=4,'c'=2] {'zh'}, dimensions={0} | all-to-all | bytes 589824 | tf_op jit(solution)/shard_map/all_to_all | solution.py:18
  78.0 2.2 %all_gather.11 = bf16[8,3,32,384]{3,2,1,0:T(8,128)(2,1)S(1)} all-gather(bf16[4,3,32,384]{3,2,1,0:T(8,128)(2,1)S(1)} %all_to_all.33), channel_id=1, replica_groups=mesh['zl'=2,'y'=8,'x'=4,'zh'=4,'c'=2] {'c'}, dimensions={0}, use_global_device_ids=true | all-gather | bytes 884736 | tf_op jit(solution)/shard_map/all_gather | solution.py:182
  80.3 0.4 convolution_convert_fusion
  80.6 0.4 fusion.8
  81.0 0.4 fusion
  81.4 1.1 pad_maximum_fusion.1
  82.5 5.3 %all-to-all-start.4 = ((bf16[8,2,48,768]{3,2,1,0:T(8,128)(2,1)}), bf16[8,2,48,768]{3,2,1,0:T(8,128)(2,1)S(1)}, u32[]{:S(2)}, u32[]{:S(2)}) async-start(bf16[8,2,48,768]{3,2,1,0:T(8,128)(2,1)} %pad_maximum_fusion.1), calls=%async_computation.4 | async-start | bytes 2359296 | tf_op jit(solution)/shard_map/all_to_all | solution.py:18
  87.9 1.1 convolution_convert_fusion.1
  89.0 1.2 convolution_convert_fusion.2
  90.2 1.2 convolution_convert_fusion.3
  91.3 11.8 %all-to-all-done.4.pieces_ref = bf16[8,2,48,768]{3,2,1,0:T(8,128)(2,1)S(1)} async-done(((bf16[8,2,48,768]{3,2,1,0:T(8,128)(2,1)}), bf16[8,2,48,768]{3,2,1,0:T(8,128)(2,1)S(1)}, u32[]{:S(2)}, u32[]{:S(2)}) %all-to-all-start.4) | async-done | bytes 1179680 | tf_op jit(solution)/shard_map/all_to_all | solution.py:18
  103.2 0.3 shard_map.111
  103.6 13.0 %all_to_all.34.pieces_ref = bf16[8,12,768]{2,1,0:T(8,128)(2,1)S(1)} all-to-all(bf16[8,12,768]{2,1,0:T(8,128)(2,1)S(1)} %shard_map.111), channel_id=1, replica_groups=mesh['zl'=2,'y'=8,'x'=4,'zh'=4,'c'=2] {'y'}, dimensions={0} | all-to-all | bytes 294912 | tf_op jit(solution)/shard_map/all_to_all | solution.py:18
  116.6 1.0 shard_map.112
  (27 shorter events, 0.8 us)
Async XLA Ops:
  0.6 39.7 %copy-start = (bf16[1,256,768]{2,1,0:T(8,128)(2,1)S(1)}, bf16[1,256,768]{2,1,0:T(8,128)(2,1)}, u32[]{:S(2)}) copy-start(bf16[1,256,768]{2,1,0:T(8,128)(2,1)} %param.11) | copy-start | bytes 1179652
  39.5 0.8 copy-start.1
  82.5 5.3 %copy-start.3 = (f32[1,1,6]{2,1,0:T(1,128)S(1)}, f32[1,1,6]{2,1,0:T(1,128)}, u32[]{:S(2)}) copy-start(f32[1,1,6]{2,1,0:T(1,128)} %param.13) | copy-start | bytes 76
  82.5 5.3 %copy-start.4 = (s32[1,1,6]{2,1,0:T(1,128)S(1)}, s32[1,1,6]{2,1,0:T(1,128)}, u32[]{:S(2)}) copy-start(s32[1,1,6]{2,1,0:T(1,128)} %param.12) | copy-start | bytes 76
  82.5 5.4 %copy-start.2 = (bf16[8,1,48,768]{3,2,1,0:T(8,128)(2,1)S(1)}, bf16[8,1,48,768]{3,2,1,0:T(8,128)(2,1)}, u32[]{:S(2)}) copy-start(bf16[8,1,48,768]{3,2,1,0:T(8,128)(2,1)} %copy-done.1) | copy-start | bytes 1769476
  82.5 20.7 %all-to-all-start.4 = ((bf16[8,2,48,768]{3,2,1,0:T(8,128)(2,1)}), bf16[8,2,48,768]{3,2,1,0:T(8,128)(2,1)S(1)}, u32[]{:S(2)}, u32[]{:S(2)}) async-start(bf16[8,2,48,768]{3,2,1,0:T(8,128)(2,1)} %pad_maximum_fusion.1), calls=%async_computation.4 | async-start | bytes 2359296 | tf_op jit(solution)/shard_map/all_to_all | solution.py:18

commit v6 on v5

--- a/solution.py
+++ b/solution.py
@@ -59,14 +59,14 @@
     copies[0].wait()
     copies[1].wait()
     cap = slots_ref.shape[0]
-    count, rows, _ = out_ref.shape
-    hot = one_hot(slots_ref, (rows, tokens_ref.shape[0]), 0, 0)
-    hot_d = one_hot(slots_ref, (rows, tokens_ref.shape[0]), 0, cap)
-    scale = by_slot(weights_ref, rows, cap, 0.0)
+    count, rows, half = out_ref.shape
+    hots = [one_hot(slots_ref, (rows, tokens_ref.shape[0]), 0, k * cap) for k in range(4)]
+    scale = by_slot(weights_ref, rows, cap, 0.0) + by_slot(weights_ref, rows, 3 * cap, 0.0)
     copies[2].wait()
     copies[3].wait()
-    picked = dot(hot, tokens_ref[...], 1, 0)
-    packed = (picked + scale * dot(hot_d, cotangent_ref[...], 1, 0)).astype(BF16)
+    picked = dot(hots[0], tokens_ref[:, :half], 1, 0) + dot(hots[2], tokens_ref[:, half:], 1, 0)
+    d_rows = dot(hots[1], cotangent_ref[:, :half], 1, 0) + dot(hots[3], cotangent_ref[:, half:], 1, 0)
+    packed = (picked + scale * d_rows).astype(BF16)
     for j in range(count):
         out_ref[j] = packed
     for copy in copies[4:]:
@@ -75,29 +75,44 @@
 
 def place_body(hot_ref, scale_ref, pieces_ref, mixed_ref, grad_ref):
     tok = mixed_ref.shape[0]
+    half = pieces_ref.shape[2]
     acc = pieces_ref[0].astype(F32)
     for j in range(1, pieces_ref.shape[0]):
         acc = acc + pieces_ref[j].astype(F32)
     acc = (acc * scale_ref[:, :1]).astype(BF16)
-    mixed_ref[...] = dot(hot_ref[:tok], acc, 1, 0).astype(BF16)
-    grad_ref[...] = dot(hot_ref[tok:], acc, 1, 0).astype(BF16)
+    for p in range(2):
+        cols = slice(p * half, (p + 1) * half)
+        mixed_ref[:, cols] = dot(hot_ref[2 * p * tok : (2 * p + 1) * tok], acc, 1, 0).astype(BF16)
+        grad_ref[:, cols] = dot(hot_ref[(2 * p + 1) * tok : (2 * p + 2) * tok], acc, 1, 0).astype(BF16)
+
+
+def moves(blocks, cap, p):
+    shape = (2 * blocks * cap, 4 * blocks * cap)
+    row = lax.broadcasted_iota(jnp.int32, (shape[0], 1), 0)
+    kind = (row >= blocks * cap).astype(jnp.int32)
+    block = sum((row - kind * blocks * cap >= b * cap).astype(jnp.int32) for b in range(1, blocks))
+    at = row + block * 3 * cap + 2 * p * cap + kind * (cap - blocks * cap)
+    return (lax.broadcasted_iota(jnp.int32, shape, 1) == at).astype(F32).astype(BF16)
+
+
+def near_body(pieces_ref, out_ref):
+    blocks, rows, half = pieces_ref.shape
+    count, _, kept, d = out_ref.shape
+    pieces = pieces_ref[...].reshape(blocks * rows, half)
+    both = [dot(moves(blocks, rows // 4, p), pieces, 1, 0).astype(BF16) for p in range(2)]
+    both = jnp.concatenate(both, axis=1).reshape(2, kept, d)
+    for j in range(count):
+        out_ref[j] = both
 
 
 def regroup_body(pieces_ref, out_ref):
-    targets, rows, d = out_ref.shape
-    cap = rows // 2
-    padded = -(-rows // 8) * 8
+    blocks, rows, half = out_ref.shape
     acc = pieces_ref[0].astype(F32)
     for j in range(1, pieces_ref.shape[0]):
         acc = acc + pieces_ref[j].astype(F32)
-    acc = acc.reshape(targets * rows, d).astype(BF16)
-    shape = (targets * padded, targets * rows)
-    at = lax.broadcasted_iota(jnp.int32, shape, 0)
-    target, row = at // padded, at % padded
-    source = jnp.where(row < cap, target * cap + row, (targets - 1 + target) * cap + row)
-    source = jnp.where(row < rows, source, -1)
-    move = (lax.broadcasted_iota(jnp.int32, shape, 1) == source).astype(F32).astype(BF16)
-    out_ref[...] = dot(move, acc, 1, 0).astype(BF16).reshape(targets, padded, d)[:, :rows]
+    acc = acc.reshape(-1, 2 * half).astype(BF16)
+    out = sum(dot(moves(blocks, rows // 4, p), acc[:, p * half : (p + 1) * half], 0, 0) for p in range(2))
+    out_ref[...] = out.astype(BF16).reshape(out_ref.shape)
 
 
 VMEM = pl.BlockSpec(memory_space=pltpu.VMEM)
@@ -110,7 +125,7 @@
         in_specs=[ANY] * 6,
         out_specs=(VMEM, VMEM, VMEM),
         out_shape=(
-            pltpu.VMEM((copies, 2 * slots.shape[0], tokens.shape[1]), BF16),
+            pltpu.VMEM((copies, 4 * slots.shape[0], tokens.shape[1] // 2), BF16),
             *(pltpu.VMEM(w.shape, BF16) for w in matrices),
         ),
         scratch_shapes=[
@@ -130,15 +145,15 @@
 
 
 def spots(slots, weights, tok):
-    cap = slots.shape[0]
-    spot = jnp.concatenate([slots, jnp.where(slots >= 0, slots + tok, -1)])
-    hot = (jnp.arange(2 * tok, dtype=jnp.int32)[:, None] == spot[None, :]).astype(BF16)
-    scale = jnp.concatenate([weights, jnp.ones((cap,), F32)])
-    return hot, jnp.broadcast_to(scale[:, None], (2 * cap, 128))
+    used = slots >= 0
+    spot = jnp.concatenate([jnp.where(used, slots + k * tok, -1) for k in range(4)])
+    hot = (jnp.arange(4 * tok, dtype=jnp.int32)[:, None] == spot[None, :]).astype(BF16)
+    scale = jnp.concatenate([weights, jnp.ones_like(weights), weights, jnp.ones_like(weights)])
+    return hot, jnp.broadcast_to(scale[:, None], (scale.shape[0], 128))
 
 
 def place(hot, scale, pieces):
-    out = jax.ShapeDtypeStruct((hot.shape[0] // 2, pieces.shape[2]), BF16)
+    out = jax.ShapeDtypeStruct((hot.shape[0] // 4, 2 * pieces.shape[2]), BF16)
     return pl.pallas_call(place_body, in_specs=[VMEM, VMEM, VMEM], out_specs=(VMEM, VMEM), out_shape=(out, out))(
         *(pltpu.with_memory_space_constraint(x, pltpu.VMEM) for x in (hot, scale, pieces))
     )
@@ -158,9 +173,7 @@
     (near, w_gate, w_up), other, kept_at, sent_at = lax.optimization_barrier(
         (pick(slots, weights, tokens, cotangent, (w_gate, w_up), 8), other, kept_at, sent_at)
     )
-    near = exchange(near, "y")
-    near = near.reshape(8, 2, cap, d).transpose(1, 0, 2, 3).reshape(2, 8 * cap, d)
-    rows = spread(near, ("zl", "x"), 8)
+    rows = exchange(on_chip(near_body, (8, 2, 8 * cap, d), BF16, exchange(near, "y")), ("zl", "x"))
     n = 64 * cap
 
     all_rows, all_grads = (rows[:, i].reshape(n, d) for i in range(2))
@@ -194,7 +207,7 @@
     both, grad_gate, grad_up, grad_down, (hot, scale) = lax.optimization_barrier(
         (both, grad_gate, grad_up, grad_down, spots(slots, weights, tok))
     )
-    both = on_chip(regroup_body, (8, 2 * cap, d), BF16, both)
+    both = on_chip(regroup_body, (8, 4 * cap, d // 2), BF16, both)
     mixed, grad_tokens = place(hot, scale, exchange(both, "y"))
     return mixed, grad_tokens, grad_gate[None], grad_up[None], grad_down[None]
 

time: 118 us -> 116 us (0.983)
  blocking collectives: 89 us -> 86.6 us
    all_to_all x5, blocking collectives: 84.6 us -> 82.2 us  [exchange(): return lax.all_to_all(pieces, axes, split_axis=0, concat_axis=0, tiled=True)]
where the time goes in v6:
time: 116 us; the launch traced here: 115 us
  blocking collectives  86.6 us (75%)
  waiting for transfers between devices  11.8 us (10%)
  matrix products  5.71 us (5%)
  starting transfers between devices  5.27 us (5%)
  Pallas kernels  3.03 us (3%)
  other arithmetic  1.62 us (1%)
    all_to_all x5, blocking collectives, exchange(): return lax.all_to_all(pieces, axes, split_axis=0, concat_axis=0, tiled=True)  82.2 us
    all_to_all x1, waiting for transfers between devices, exchange(): return lax.all_to_all(pieces, axes, split_axis=0, concat_axis=0, tiled=True)  11.8 us
    dot_general x9, matrix products, dot(): lax.dot_general(a, b, (((ca,), (cb,)), ((), ())), preferred_element_type=...  5.71 us
    all_to_all x1, starting transfers between devices, exchange(): return lax.all_to_all(pieces, axes, split_axis=0, concat_axis=0, tiled=True)  5.27 us
  transfers between devices with their start and end apart: 1, of which 1 were waited for; matrix products, arithmetic and copies ran while one was open for 3% of the time, Pallas kernels for 0%

profile of v6, /device:TPU:6, one launch (start us, length us, event | category | flops | bytes accessed | tf_op | source)
XLA Modules:
  0.0 115.2 jit_solution(1870215870594086775)
XLA Ops:
  0.7 1.4 %shard_map.110 = (bf16[8,24,384]{2,1,0:T(8,128)(2,1)S(1)}, bf16[768,256]{1,0:T(8,128)(2,1)S(1)}, bf16[768,256]{1,0:T(8,128)(2,1)S(1)}) custom-call(s32[6]{0:T(128)} %bitcast.95, f32[6]{0:T(128)} %bitcast.97, bf16[128,768]{1,0:T(8,128)(2,1)} %refs_2_.1, bf16[128,768]{1,0:T(8,128)(2,1)} %refs_3_.1, bf16[768,256]{1,0:T(8,128)(2,1)} %bitcast.90, ...), custom_call_target="tpu_custom_call" | custom-call | tf_op jit(solution)/shard_map/pallas_call | solution.py:123
  2.1 16.3 %all_to_all.30.pieces_ref = bf16[8,24,384]{2,1,0:T(8,128)(2,1)S(1)} all-to-all(bf16[8,24,384]{2,1,0:T(8,128)(2,1)S(1)} %get-tuple-element.29), channel_id=1, replica_groups=mesh['zl'=2,'y'=8,'x'=4,'zh'=4,'c'=2] {'y'}, dimensions={0} | all-to-all | bytes 294912 | tf_op jit(solution)/shard_map/all_to_all | solution.py:18
  18.4 0.2 shard_map.111
  18.6 19.6 %all_to_all.31 = bf16[8,2,48,768]{3,2,1,0:T(8,128)(2,1)S(1)} all-to-all(bf16[8,2,48,768]{3,2,1,0:T(8,128)(2,1)S(1)} %shard_map.111), channel_id=1, replica_groups=mesh['zl'=2,'y'=8,'x'=4,'zh'=4,'c'=2] {'zl','x'}, dimensions={0} | all-to-all | bytes 2359296 | tf_op jit(solution)/shard_map/all_to_all | solution.py:18
  38.3 0.4 convolution_bitcast_fusion.2
  38.7 0.4 convolution_bitcast_fusion.1
  39.2 0.4 convolution_bitcast_fusion
  39.7 2.2 %all-gather = bf16[6,128,384]{2,1,0:T(8,128)(2,1)S(1)} all-gather(bf16[3,128,384]{2,1,0:T(8,128)(2,1)S(1)} %dynamic-slice_convert_fusion), channel_id=2, replica_groups=mesh['zl'=2,'y'=8,'x'=4,'zh'=4,'c'=2] {'c'}, dimensions={0}, use_global_device_ids=true | all-gather | bytes 884736 | tf_op jit(solution)/shard_map/all_gather | solution.py:181
  41.9 0.1 fusion.1
  42.1 21.3 %all_to_all.32 = bf16[4,3,32,384]{3,2,1,0:T(8,128)(2,1)S(1)} all-to-all(bf16[4,3,32,384]{3,2,1,0:T(8,128)(2,1)S(1)} %bitcast.88), channel_id=1, replica_groups=mesh['zl'=2,'y'=8,'x'=4,'zh'=4,'c'=2] {'zh'}, dimensions={0} | all-to-all | bytes 589824 | tf_op jit(solution)/shard_map/all_to_all | solution.py:18
  63.6 13.2 %all_to_all.33 = bf16[4,3,32,384]{3,2,1,0:T(8,128)(2,1)S(1)} all-to-all(bf16[4,3,32,384]{3,2,1,0:T(8,128)(2,1)S(1)} %broadcast_in_dim.30), channel_id=1, replica_groups=mesh['zl'=2,'y'=8,'x'=4,'zh'=4,'c'=2] {'zh'}, dimensions={0} | all-to-all | bytes 589824 | tf_op jit(solution)/shard_map/all_to_all | solution.py:18
  76.8 2.2 %all_gather.11 = bf16[8,3,32,384]{3,2,1,0:T(8,128)(2,1)S(1)} all-gather(bf16[4,3,32,384]{3,2,1,0:T(8,128)(2,1)S(1)} %all_to_all.33), channel_id=1, replica_groups=mesh['zl'=2,'y'=8,'x'=4,'zh'=4,'c'=2] {'c'}, dimensions={0}, use_global_device_ids=true | all-gather | bytes 884736 | tf_op jit(solution)/shard_map/all_gather | solution.py:195
  79.1 0.4 fusion.8
  79.5 0.4 convolution_convert_fusion
  79.9 0.4 fusion
  80.3 1.1 pad_maximum_fusion.1
  81.4 5.3 %all-to-all-start.4 = ((bf16[8,2,48,768]{3,2,1,0:T(8,128)(2,1)}), bf16[8,2,48,768]{3,2,1,0:T(8,128)(2,1)S(1)}, u32[]{:S(2)}, u32[]{:S(2)}) async-start(bf16[8,2,48,768]{3,2,1,0:T(8,128)(2,1)} %pad_maximum_fusion.1), calls=%async_computation.4 | async-start | bytes 2359296 | tf_op jit(solution)/shard_map/all_to_all | solution.py:18
  86.9 1.1 convolution_convert_fusion.1
  88.0 1.2 convolution_convert_fusion.2
  89.2 1.1 convolution_convert_fusion.3
  90.3 11.8 %all-to-all-done.4.pieces_ref = bf16[8,2,48,768]{3,2,1,0:T(8,128)(2,1)S(1)} async-done(((bf16[8,2,48,768]{3,2,1,0:T(8,128)(2,1)}), bf16[8,2,48,768]{3,2,1,0:T(8,128)(2,1)S(1)}, u32[]{:S(2)}, u32[]{:S(2)}) %all-to-all-start.4) | async-done | bytes 1179680 | tf_op jit(solution)/shard_map/all_to_all | solution.py:18
  102.2 0.4 shard_map.112
  102.5 11.6 %all_to_all.34.pieces_ref = bf16[8,24,384]{2,1,0:T(8,128)(2,1)S(1)} all-to-all(bf16[8,24,384]{2,1,0:T(8,128)(2,1)S(1)} %shard_map.112), channel_id=1, replica_groups=mesh['zl'=2,'y'=8,'x'=4,'zh'=4,'c'=2] {'y'}, dimensions={0} | all-to-all | bytes 294912 | tf_op jit(solution)/shard_map/all_to_all | solution.py:18
  114.2 1.0 shard_map.113
  (25 shorter events, 0.7 us)
Async XLA Ops:
  0.6 38.5 %copy-start = (bf16[1,256,768]{2,1,0:T(8,128)(2,1)S(1)}, bf16[1,256,768]{2,1,0:T(8,128)(2,1)}, u32[]{:S(2)}) copy-start(bf16[1,256,768]{2,1,0:T(8,128)(2,1)} %param.11) | copy-start | bytes 1179652
  79.1 0.8 copy-start.1
  81.4 5.3 %copy-start.4 = (f32[1,1,6]{2,1,0:T(1,128)S(1)}, f32[1,1,6]{2,1,0:T(1,128)}, u32[]{:S(2)}) copy-start(f32[1,1,6]{2,1,0:T(1,128)} %param.13) | copy-start | bytes 76
  81.4 5.4 %copy-start.3 = (s32[1,1,6]{2,1,0:T(1,128)S(1)}, s32[1,1,6]{2,1,0:T(1,128)}, u32[]{:S(2)}) copy-start(s32[1,1,6]{2,1,0:T(1,128)} %param.12) | copy-start | bytes 76
  81.4 5.5 %copy-start.2 = (bf16[8,1,32,384]{3,2,1,0:T(8,128)(2,1)S(1)}, bf16[8,1,32,384]{3,2,1,0:T(8,128)(2,1)}, u32[]{:S(2)}) copy-start(bf16[8,1,32,384]{3,2,1,0:T(8,128)(2,1)} %copy-done.1) | copy-start | bytes 589828
  81.4 20.7 %all-to-all-start.4 = ((bf16[8,2,48,768]{3,2,1,0:T(8,128)(2,1)}), bf16[8,2,48,768]{3,2,1,0:T(8,128)(2,1)S(1)}, u32[]{:S(2)}, u32[]{:S(2)}) async-start(bf16[8,2,48,768]{3,2,1,0:T(8,128)(2,1)} %pad_maximum_fusion.1), calls=%async_computation.4 | async-start | bytes 2359296 | tf_op jit(solution)/shard_map/all_to_all | solution.py:18

commit v7 on v6

--- a/solution.py
+++ b/solution.py
@@ -73,17 +73,22 @@
         copy.wait()
 
 
-def place_body(hot_ref, scale_ref, pieces_ref, mixed_ref, grad_ref):
-    tok = mixed_ref.shape[0]
+def place_body(hot_ref, scale_ref, pieces_ref, *refs):
     half = pieces_ref.shape[2]
+    tok = hot_ref.shape[0] // 4
     acc = pieces_ref[0].astype(F32)
     for j in range(1, pieces_ref.shape[0]):
         acc = acc + pieces_ref[j].astype(F32)
     acc = (acc * scale_ref[:, :1]).astype(BF16)
-    for p in range(2):
-        cols = slice(p * half, (p + 1) * half)
-        mixed_ref[:, cols] = dot(hot_ref[2 * p * tok : (2 * p + 1) * tok], acc, 1, 0).astype(BF16)
-        grad_ref[:, cols] = dot(hot_ref[(2 * p + 1) * tok : (2 * p + 2) * tok], acc, 1, 0).astype(BF16)
+    sems = refs[4]
+    copies = [pltpu.make_async_copy(refs[2 + k], refs[k], sems.at[k]) for k in range(2)]
+    for k in range(2):
+        for p in range(2):
+            hot = hot_ref[(2 * p + k) * tok : (2 * p + k + 1) * tok]
+            refs[2 + k][:, p * half : (p + 1) * half] = dot(hot, acc, 1, 0).astype(BF16)
+        copies[k].start()
+    for copy in copies:
+        copy.wait()
 
 
 def moves(blocks, cap, p):
@@ -103,6 +108,19 @@
     both = jnp.concatenate(both, axis=1).reshape(2, kept, d)
     for j in range(count):
         out_ref[j] = both
+
+
+def slot_body(out_ref, full_ref, w_gate_ref, w_up_ref, both_ref, back_ref, sems):
+    first = pltpu.make_async_copy(out_ref, both_ref.at[:, 0], sems.at[0])
+    first.start()
+    n = full_ref.shape[3]
+    d_gate, d_up = (full_ref[:, i].reshape(-1, n).T for i in (1, 2))
+    back = dot(d_gate, w_gate_ref[...], 1, 1) + dot(d_up, w_up_ref[...], 1, 1)
+    back_ref[...] = back.astype(BF16).reshape(back_ref.shape)
+    second = pltpu.make_async_copy(back_ref, both_ref.at[:, 1], sems.at[1])
+    second.start()
+    first.wait()
+    second.wait()
 
 
 def regroup_body(pieces_ref, out_ref):
@@ -144,6 +162,17 @@
     )(*(pltpu.with_memory_space_constraint(x, pltpu.VMEM) for x in arrays))
 
 
+def pair(out, full, w_gate, w_up):
+    groups, rows, d = out.shape
+    return pl.pallas_call(
+        slot_body,
+        in_specs=[VMEM] * 4,
+        out_specs=ANY,
+        out_shape=jax.ShapeDtypeStruct((groups, 2, rows, d), BF16),
+        scratch_shapes=[pltpu.VMEM(out.shape, BF16), pltpu.SemaphoreType.DMA((2,))],
+    )(*(pltpu.with_memory_space_constraint(x, pltpu.VMEM) for x in (out, full, w_gate, w_up)))
+
+
 def spots(slots, weights, tok):
     used = slots >= 0
     spot = jnp.concatenate([jnp.where(used, slots + k * tok, -1) for k in range(4)])
@@ -154,9 +183,13 @@
 
 def place(hot, scale, pieces):
     out = jax.ShapeDtypeStruct((hot.shape[0] // 4, 2 * pieces.shape[2]), BF16)
-    return pl.pallas_call(place_body, in_specs=[VMEM, VMEM, VMEM], out_specs=(VMEM, VMEM), out_shape=(out, out))(
-        *(pltpu.with_memory_space_constraint(x, pltpu.VMEM) for x in (hot, scale, pieces))
-    )
+    return pl.pallas_call(
+        place_body,
+        in_specs=[VMEM] * 3,
+        out_specs=(ANY, ANY),
+        out_shape=(out, out),
+        scratch_shapes=[pltpu.VMEM(out.shape, BF16), pltpu.VMEM(out.shape, BF16), pltpu.SemaphoreType.DMA((2,))],
+    )(*(pltpu.with_memory_space_constraint(x, pltpu.VMEM) for x in (hot, scale, pieces)))
 
 
 def on_device(tokens, cotangent, w_gate, w_up, w_down, slot_token, route_weight):
@@ -196,8 +229,7 @@
 
     hidden, d_gate, d_up = (full[:, i].reshape(ff, n) for i in range(3))
     out = dot(hidden, w_down, 0, 0).astype(BF16)
-    back = (dot(d_gate, w_gate, 0, 1) + dot(d_up, w_up, 0, 1)).astype(BF16)
-    both = jnp.stack([out.reshape(8, 8 * cap, d), back.reshape(8, 8 * cap, d)], axis=1)
+    both = pair(out.reshape(8, 8 * cap, d), full, w_gate, w_up)
     both, slots, weights = lax.optimization_barrier((both, slots, weights))
     both = exchange(both, ("zl", "x"))
 

time: 116 us -> 115 us (level)
  Pallas kernels: 3.03 us -> 4.35 us
    pallas_call x1 -> x2, Pallas kernels: 1.04 us -> 2.35 us  [the longest x1 1.34 us: pair(): pl.pallas_call(slot_body, in_specs=[VMEM] * 4, out_specs=ANY, out_shape=j...]
    dot_general x9 -> x7, matrix products: 5.71 us -> 4.97 us  [dot(): lax.dot_general(a, b, (((ca,), (cb,)), ((), ())), preferred_element_type=...]
where the time goes in v7:
time: 115 us
  blocking collectives  86.7 us (75%)
  waiting for transfers between devices  11.8 us (10%)
  starting transfers between devices  5.28 us (5%)
  matrix products  4.97 us (4%)
  Pallas kernels  4.35 us (4%)
    all_to_all x5, blocking collectives, exchange(): return lax.all_to_all(pieces, axes, split_axis=0, concat_axis=0, tiled=True)  82.2 us
    all_to_all x1, waiting for transfers between devices, exchange(): return lax.all_to_all(pieces, axes, split_axis=0, concat_axis=0, tiled=True)  11.8 us
    all_to_all x1, starting transfers between devices, exchange(): return lax.all_to_all(pieces, axes, split_axis=0, concat_axis=0, tiled=True)  5.28 us
    dot_general x7, matrix products, dot(): lax.dot_general(a, b, (((ca,), (cb,)), ((), ())), preferred_element_type=...  4.97 us
  transfers between devices with their start and end apart: 1, of which 1 were waited for; matrix products, arithmetic and copies ran while one was open for 3% of the time, Pallas kernels for 0%

profile of v7, /device:TPU:6, one launch (start us, length us, event | category | flops | bytes accessed | tf_op | source)
XLA Modules:
  0.0 114.7 jit_solution(10349893178276030968)
XLA Ops:
  0.7 1.4 %shard_map.110 = (bf16[8,24,384]{2,1,0:T(8,128)(2,1)S(1)}, bf16[768,256]{1,0:T(8,128)(2,1)S(1)}, bf16[768,256]{1,0:T(8,128)(2,1)S(1)}) custom-call(s32[6]{0:T(128)} %bitcast.87, f32[6]{0:T(128)} %bitcast.89, bf16[128,768]{1,0:T(8,128)(2,1)} %refs_2_.1, bf16[128,768]{1,0:T(8,128)(2,1)} %refs_3_.1, bf16[768,256]{1,0:T(8,128)(2,1)} %bitcast.82, ...), custom_call_target="tpu_custom_call" | custom-call | tf_op jit(solution)/shard_map/pallas_call | solution.py:141
  2.1 16.3 %all_to_all.30.pieces_ref = bf16[8,24,384]{2,1,0:T(8,128)(2,1)S(1)} all-to-all(bf16[8,24,384]{2,1,0:T(8,128)(2,1)S(1)} %get-tuple-element.29), channel_id=1, replica_groups=mesh['zl'=2,'y'=8,'x'=4,'zh'=4,'c'=2] {'y'}, dimensions={0} | all-to-all | bytes 294912 | tf_op jit(solution)/shard_map/all_to_all | solution.py:18
  18.4 0.2 shard_map.111
  18.6 19.6 %all_to_all.31 = bf16[8,2,48,768]{3,2,1,0:T(8,128)(2,1)S(1)} all-to-all(bf16[8,2,48,768]{3,2,1,0:T(8,128)(2,1)S(1)} %shard_map.111), channel_id=1, replica_groups=mesh['zl'=2,'y'=8,'x'=4,'zh'=4,'c'=2] {'zl','x'}, dimensions={0} | all-to-all | bytes 2359296 | tf_op jit(solution)/shard_map/all_to_all | solution.py:18
  38.3 0.4 convolution_bitcast_fusion.1
  38.8 0.4 convolution_bitcast_fusion.2
  39.2 0.4 convolution_bitcast_fusion
  39.6 0.1 pad_maximum_fusion
  39.7 2.2 %all-gather = bf16[6,128,384]{2,1,0:T(8,128)(2,1)S(1)} all-gather(bf16[3,128,384]{2,1,0:T(8,128)(2,1)S(1)} %dynamic-slice_convert_fusion), channel_id=2, replica_groups=mesh['zl'=2,'y'=8,'x'=4,'zh'=4,'c'=2] {'c'}, dimensions={0}, use_global_device_ids=true | all-gather | bytes 884736 | tf_op jit(solution)/shard_map/all_gather | solution.py:214
  42.0 0.1 fusion
  42.1 21.4 %all_to_all.32 = bf16[4,3,32,384]{3,2,1,0:T(8,128)(2,1)S(1)} all-to-all(bf16[4,3,32,384]{3,2,1,0:T(8,128)(2,1)S(1)} %bitcast.78), channel_id=1, replica_groups=mesh['zl'=2,'y'=8,'x'=4,'zh'=4,'c'=2] {'zh'}, dimensions={0} | all-to-all | bytes 589824 | tf_op jit(solution)/shard_map/all_to_all | solution.py:18
  63.6 13.2 %all_to_all.33 = bf16[4,3,32,384]{3,2,1,0:T(8,128)(2,1)S(1)} all-to-all(bf16[4,3,32,384]{3,2,1,0:T(8,128)(2,1)S(1)} %broadcast_in_dim.30), channel_id=1, replica_groups=mesh['zl'=2,'y'=8,'x'=4,'zh'=4,'c'=2] {'zh'}, dimensions={0} | all-to-all | bytes 589824 | tf_op jit(solution)/shard_map/all_to_all | solution.py:18
  76.8 2.2 %all_gather.11.full_ref = bf16[8,3,32,384]{3,2,1,0:T(8,128)(2,1)S(1)} all-gather(bf16[4,3,32,384]{3,2,1,0:T(8,128)(2,1)S(1)} %all_to_all.33), channel_id=1, replica_groups=mesh['zl'=2,'y'=8,'x'=4,'zh'=4,'c'=2] {'c'}, dimensions={0}, use_global_device_ids=true | all-gather | bytes 884736 | tf_op jit(solution)/shard_map/all_gather | solution.py:228
  79.1 0.4 convolution_convert_fusion
  79.5 1.3 %shard_map.112 = bf16[8,2,48,768]{3,2,1,0:T(8,128)(2,1)} custom-call(bf16[8,48,768]{2,1,0:T(8,128)(2,1)S(1)} %bitcast.68, bf16[8,3,32,384]{3,2,1,0:T(8,128)(2,1)S(1)} %all_gather.11.full_ref, bf16[768,256]{1,0:T(8,128)(2,1)S(1)} %get-tuple-element.28.w_gate_ref, bf16[768,256]{1,0:T(8,128)(2,1)S(1)} %get-tuple-element.30.w_up_ref), custom_call_target="tpu_custom_call" | custom-call | tf_op jit(solution)/shard_map/pallas_call | solution.py:167
  80.9 5.3 %all-to-all-start.4 = ((bf16[8,2,48,768]{3,2,1,0:T(8,128)(2,1)}), bf16[8,2,48,768]{3,2,1,0:T(8,128)(2,1)S(1)}, u32[]{:S(2)}, u32[]{:S(2)}) async-start(bf16[8,2,48,768]{3,2,1,0:T(8,128)(2,1)} %shard_map.112), calls=%async_computation.4 | async-start | bytes 2359296 | tf_op jit(solution)/shard_map/all_to_all | solution.py:18
  86.3 0.1 pad_add_fusion
  86.4 1.1 convolution_convert_fusion.1
  87.5 1.1 %convolution_convert_fusion.3 = bf16[768,256]{1,0:T(8,128)(2,1)} fusion(bf16[384,768]{1,0:T(8,128)(2,1)S(1)} %bitcast.71, bf16[256,384]{1,0:T(8,128)(2,1)S(1)} %bitcast.81), kind=kOutput, calls=%fused_computation.3 | convolution fusion | flops 151191552 | bytes 1179648 | tf_op jit(solution)/shard_map/dot_general | solution.py:33
  88.7 1.2 %convolution_convert_fusion.2 = bf16[768,256]{1,0:T(8,128)(2,1)} fusion(bf16[384,768]{1,0:T(8,128)(2,1)S(1)} %bitcast.72, bf16[256,384]{1,0:T(8,128)(2,1)S(1)} %bitcast.80), kind=kOutput, calls=%fused_computation.2 | convolution fusion | flops 151191552 | bytes 1179648 | tf_op jit(solution)/shard_map/dot_general | solution.py:33
  89.8 11.8 %all-to-all-done.4.pieces_ref = bf16[8,2,48,768]{3,2,1,0:T(8,128)(2,1)S(1)} async-done(((bf16[8,2,48,768]{3,2,1,0:T(8,128)(2,1)}), bf16[8,2,48,768]{3,2,1,0:T(8,128)(2,1)S(1)}, u32[]{:S(2)}, u32[]{:S(2)}) %all-to-all-start.4) | async-done | bytes 1179680 | tf_op jit(solution)/shard_map/all_to_all | solution.py:18
  101.6 0.4 shard_map.113
  102.0 11.7 %all_to_all.34.pieces_ref = bf16[8,24,384]{2,1,0:T(8,128)(2,1)S(1)} all-to-all(bf16[8,24,384]{2,1,0:T(8,128)(2,1)S(1)} %shard_map.113), channel_id=1, replica_groups=mesh['zl'=2,'y'=8,'x'=4,'zh'=4,'c'=2] {'y'}, dimensions={0} | all-to-all | bytes 294912 | tf_op jit(solution)/shard_map/all_to_all | solution.py:18
  113.7 1.0 shard_map.114
  (23 shorter events, 0.6 us)
Async XLA Ops:
  0.6 38.5 %copy-start = (bf16[1,256,768]{2,1,0:T(8,128)(2,1)S(1)}, bf16[1,256,768]{2,1,0:T(8,128)(2,1)}, u32[]{:S(2)}) copy-start(bf16[1,256,768]{2,1,0:T(8,128)(2,1)} %param.11) | copy-start | bytes 1179652
  38.3 0.8 copy-start.1
  80.9 5.3 %copy-start.4 = (f32[1,1,6]{2,1,0:T(1,128)S(1)}, f32[1,1,6]{2,1,0:T(1,128)}, u32[]{:S(2)}) copy-start(f32[1,1,6]{2,1,0:T(1,128)} %param.13) | copy-start | bytes 76
  80.9 5.4 %copy-start.3 = (s32[1,1,6]{2,1,0:T(1,128)S(1)}, s32[1,1,6]{2,1,0:T(1,128)}, u32[]{:S(2)}) copy-start(s32[1,1,6]{2,1,0:T(1,128)} %param.12) | copy-start | bytes 76
  80.9 5.5 %copy-start.2 = (bf16[8,1,48,768]{3,2,1,0:T(8,128)(2,1)S(1)}, bf16[8,1,48,768]{3,2,1,0:T(8,128)(2,1)}, u32[]{:S(2)}) copy-start(bf16[8,1,48,768]{3,2,1,0:T(8,128)(2,1)} %copy-done.1) | copy-start | bytes 1769476
  80.9 20.7 %all-to-all-start.4 = ((bf16[8,2,48,768]{3,2,1,0:T(8,128)(2,1)}), bf16[8,2,48,768]{3,2,1,0:T(8,128)(2,1)S(1)}, u32[]{:S(2)}, u32[]{:S(2)}) async-start(bf16[8,2,48,768]{3,2,1,0:T(8,128)(2,1)} %shard_map.112), calls=%async_computation.4 | async-start | bytes 2359296 | tf_op jit(solution)/shard_map/all_to_all | solution.py:18

commit v8 on v7

--- a/solution.py
+++ b/solution.py
@@ -111,16 +111,33 @@
 
 
 def slot_body(out_ref, full_ref, w_gate_ref, w_up_ref, both_ref, back_ref, sems):
-    first = pltpu.make_async_copy(out_ref, both_ref.at[:, 0], sems.at[0])
-    first.start()
+    copies = [pltpu.make_async_copy(out_ref, both_ref.at[:, 0], sems.at[0])]
+    copies[0].start()
+    groups, rows, d = out_ref.shape
     n = full_ref.shape[3]
     d_gate, d_up = (full_ref[:, i].reshape(-1, n).T for i in (1, 2))
-    back = dot(d_gate, w_gate_ref[...], 1, 1) + dot(d_up, w_up_ref[...], 1, 1)
-    back_ref[...] = back.astype(BF16).reshape(back_ref.shape)
-    second = pltpu.make_async_copy(back_ref, both_ref.at[:, 1], sems.at[1])
-    second.start()
-    first.wait()
-    second.wait()
+    part = groups // 2
+    for j in range(2):
+        here = pl.ds(j * part, part)
+        take = slice(j * part * rows, (j + 1) * part * rows)
+        back = dot(d_gate[take], w_gate_ref[...], 1, 1) + dot(d_up[take], w_up_ref[...], 1, 1)
+        back_ref[here] = back.astype(BF16).reshape(part, rows, d)
+        copies.append(pltpu.make_async_copy(back_ref.at[here], both_ref.at[here, 1], sems.at[1 + j]))
+        copies[-1].start()
+    for copy in copies:
+        copy.wait()
+
+
+def spot_body(slots_ref, weights_ref, hot_ref, scale_ref):
+    cap = slots_ref.shape[0]
+    tok = hot_ref.shape[0] // 4
+    for k in range(4):
+        hot_ref[k * tok : (k + 1) * tok] = one_hot(slots_ref, (tok, 4 * cap), 1, k * cap)
+    slot = lax.broadcasted_iota(jnp.int32, scale_ref.shape, 0)
+    scale = jnp.ones(scale_ref.shape, F32)
+    for s in range(cap):
+        scale = jnp.where((slot == s) | (slot == 2 * cap + s), weights_ref[s], scale)
+    scale_ref[...] = scale
 
 
 def regroup_body(pieces_ref, out_ref):
@@ -133,6 +150,7 @@
     out_ref[...] = out.astype(BF16).reshape(out_ref.shape)
 
 
+SMEM = pl.BlockSpec(memory_space=pltpu.SMEM)
 VMEM = pl.BlockSpec(memory_space=pltpu.VMEM)
 ANY = pl.BlockSpec(memory_space=pl.ANY)
 
@@ -169,16 +187,18 @@
         in_specs=[VMEM] * 4,
         out_specs=ANY,
         out_shape=jax.ShapeDtypeStruct((groups, 2, rows, d), BF16),
-        scratch_shapes=[pltpu.VMEM(out.shape, BF16), pltpu.SemaphoreType.DMA((2,))],
+        scratch_shapes=[pltpu.VMEM(out.shape, BF16), pltpu.SemaphoreType.DMA((3,))],
     )(*(pltpu.with_memory_space_constraint(x, pltpu.VMEM) for x in (out, full, w_gate, w_up)))
 
 
 def spots(slots, weights, tok):
-    used = slots >= 0
-    spot = jnp.concatenate([jnp.where(used, slots + k * tok, -1) for k in range(4)])
-    hot = (jnp.arange(4 * tok, dtype=jnp.int32)[:, None] == spot[None, :]).astype(BF16)
-    scale = jnp.concatenate([weights, jnp.ones_like(weights), weights, jnp.ones_like(weights)])
-    return hot, jnp.broadcast_to(scale[:, None], (scale.shape[0], 128))
+    rows = 4 * slots.shape[0]
+    return pl.pallas_call(
+        spot_body,
+        in_specs=[SMEM, SMEM],
+        out_specs=(VMEM, VMEM),
+        out_shape=(pltpu.VMEM((4 * tok, rows), BF16), pltpu.VMEM((rows, 128), F32)),
+    )(slots, weights)
 
 
 def place(hot, scale, pieces):

time: 115 us -> 115 us (level)
  transfers between devices with their start and end apart: 1 -> 1, of which waited for: 1 -> 1; matrix products, arithmetic and copies ran while one was open for 3% -> 3% of each run, Pallas kernels for 0% -> 1%
where the time goes in v8:
time: 115 us
  blocking collectives  86.7 us (75%)
  waiting for transfers between devices  11.3 us (10%)
  starting transfers between devices  5.28 us (5%)
  Pallas kernels  5.14 us (4%)
  matrix products  4.97 us (4%)
    all_to_all x5, blocking collectives, exchange(): return lax.all_to_all(pieces, axes, split_axis=0, concat_axis=0, tiled=True)  82.2 us
    all_to_all x1, waiting for transfers between devices, exchange(): return lax.all_to_all(pieces, axes, split_axis=0, concat_axis=0, tiled=True)  11.3 us
    all_to_all x1, starting transfers between devices, exchange(): return lax.all_to_all(pieces, axes, split_axis=0, concat_axis=0, tiled=True)  5.28 us
    dot_general x7, matrix products, dot(): lax.dot_general(a, b, (((ca,), (cb,)), ((), ())), preferred_element_type=...  4.97 us
  transfers between devices with their start and end apart: 1, of which 1 were waited for; matrix products, arithmetic and copies ran while one was open for 3% of the time, Pallas kernels for 1%

profile of v8, /device:TPU:6, one launch (start us, length us, event | category | flops | bytes accessed | tf_op | source)
XLA Modules:
  0.0 114.7 jit_solution(609281928202737543)
XLA Ops:
  0.7 1.4 %shard_map.110 = (bf16[8,24,384]{2,1,0:T(8,128)(2,1)S(1)}, bf16[768,256]{1,0:T(8,128)(2,1)S(1)}, bf16[768,256]{1,0:T(8,128)(2,1)S(1)}) custom-call(s32[6]{0:T(128)} %bitcast.87, f32[6]{0:T(128)} %bitcast.89, bf16[128,768]{1,0:T(8,128)(2,1)} %refs_2_.1, bf16[128,768]{1,0:T(8,128)(2,1)} %refs_3_.1, bf16[768,256]{1,0:T(8,128)(2,1)} %bitcast.82, ...), custom_call_target="tpu_custom_call" | custom-call | tf_op jit(solution)/shard_map/pallas_call | solution.py:159
  2.1 16.3 %all_to_all.30.pieces_ref = bf16[8,24,384]{2,1,0:T(8,128)(2,1)S(1)} all-to-all(bf16[8,24,384]{2,1,0:T(8,128)(2,1)S(1)} %get-tuple-element.31), channel_id=1, replica_groups=mesh['zl'=2,'y'=8,'x'=4,'zh'=4,'c'=2] {'y'}, dimensions={0} | all-to-all | bytes 294912 | tf_op jit(solution)/shard_map/all_to_all | solution.py:18
  18.4 0.2 shard_map.111
  18.6 19.6 %all_to_all.31 = bf16[8,2,48,768]{3,2,1,0:T(8,128)(2,1)S(1)} all-to-all(bf16[8,2,48,768]{3,2,1,0:T(8,128)(2,1)S(1)} %shard_map.111), channel_id=1, replica_groups=mesh['zl'=2,'y'=8,'x'=4,'zh'=4,'c'=2] {'zl','x'}, dimensions={0} | all-to-all | bytes 2359296 | tf_op jit(solution)/shard_map/all_to_all | solution.py:18
  38.3 0.4 convolution_bitcast_fusion.1
  38.8 0.4 convolution_bitcast_fusion.2
  39.2 0.4 convolution_bitcast_fusion
  39.6 0.1 pad_maximum_fusion
  39.7 2.2 %all-gather = bf16[6,128,384]{2,1,0:T(8,128)(2,1)S(1)} all-gather(bf16[3,128,384]{2,1,0:T(8,128)(2,1)S(1)} %dynamic-slice_convert_fusion), channel_id=2, replica_groups=mesh['zl'=2,'y'=8,'x'=4,'zh'=4,'c'=2] {'c'}, dimensions={0}, use_global_device_ids=true | all-gather | bytes 884736 | tf_op jit(solution)/shard_map/all_gather | solution.py:234
  42.0 0.1 fusion
  42.1 21.4 %all_to_all.32 = bf16[4,3,32,384]{3,2,1,0:T(8,128)(2,1)S(1)} all-to-all(bf16[4,3,32,384]{3,2,1,0:T(8,128)(2,1)S(1)} %bitcast.78), channel_id=1, replica_groups=mesh['zl'=2,'y'=8,'x'=4,'zh'=4,'c'=2] {'zh'}, dimensions={0} | all-to-all | bytes 589824 | tf_op jit(solution)/shard_map/all_to_all | solution.py:18
  63.6 13.2 %all_to_all.33 = bf16[4,3,32,384]{3,2,1,0:T(8,128)(2,1)S(1)} all-to-all(bf16[4,3,32,384]{3,2,1,0:T(8,128)(2,1)S(1)} %broadcast_in_dim.15), channel_id=1, replica_groups=mesh['zl'=2,'y'=8,'x'=4,'zh'=4,'c'=2] {'zh'}, dimensions={0} | all-to-all | bytes 589824 | tf_op jit(solution)/shard_map/all_to_all | solution.py:18
  76.8 2.2 %all_gather.11.full_ref = bf16[8,3,32,384]{3,2,1,0:T(8,128)(2,1)S(1)} all-gather(bf16[4,3,32,384]{3,2,1,0:T(8,128)(2,1)S(1)} %all_to_all.33), channel_id=1, replica_groups=mesh['zl'=2,'y'=8,'x'=4,'zh'=4,'c'=2] {'c'}, dimensions={0}, use_global_device_ids=true | all-gather | bytes 884736 | tf_op jit(solution)/shard_map/all_gather | solution.py:248
  79.1 0.4 convolution_convert_fusion
  79.5 1.4 %shard_map.112 = bf16[8,2,48,768]{3,2,1,0:T(8,128)(2,1)} custom-call(bf16[8,48,768]{2,1,0:T(8,128)(2,1)S(1)} %bitcast.68, bf16[8,3,32,384]{3,2,1,0:T(8,128)(2,1)S(1)} %all_gather.11.full_ref, bf16[768,256]{1,0:T(8,128)(2,1)S(1)} %get-tuple-element.30.w_gate_ref, bf16[768,256]{1,0:T(8,128)(2,1)S(1)} %get-tuple-element.32.w_up_ref), custom_call_target="tpu_custom_call" | custom-call | tf_op jit(solution)/shard_map/pallas_call | solution.py:185
  80.9 5.3 %all-to-all-start.4 = ((bf16[8,2,48,768]{3,2,1,0:T(8,128)(2,1)}), bf16[8,2,48,768]{3,2,1,0:T(8,128)(2,1)S(1)}, u32[]{:S(2)}, u32[]{:S(2)}) async-start(bf16[8,2,48,768]{3,2,1,0:T(8,128)(2,1)} %shard_map.112), calls=%async_computation.4 | async-start | bytes 2359296 | tf_op jit(solution)/shard_map/all_to_all | solution.py:18
  86.2 0.7 shard_map.113
  86.9 1.1 convolution_convert_fusion.1
  88.1 1.2 %convolution_convert_fusion.3 = bf16[768,256]{1,0:T(8,128)(2,1)} fusion(bf16[384,768]{1,0:T(8,128)(2,1)S(1)} %bitcast.71, bf16[256,384]{1,0:T(8,128)(2,1)S(1)} %bitcast.81), kind=kOutput, calls=%fused_computation.3 | convolution fusion | flops 151191552 | bytes 1179648 | tf_op jit(solution)/shard_map/dot_general | solution.py:33
  89.2 1.2 %convolution_convert_fusion.2 = bf16[768,256]{1,0:T(8,128)(2,1)} fusion(bf16[384,768]{1,0:T(8,128)(2,1)S(1)} %bitcast.72, bf16[256,384]{1,0:T(8,128)(2,1)S(1)} %bitcast.80), kind=kOutput, calls=%fused_computation.2 | convolution fusion | flops 151191552 | bytes 1179648 | tf_op jit(solution)/shard_map/dot_general | solution.py:33
  90.4 11.3 %all-to-all-done.4.pieces_ref = bf16[8,2,48,768]{3,2,1,0:T(8,128)(2,1)S(1)} async-done(((bf16[8,2,48,768]{3,2,1,0:T(8,128)(2,1)}), bf16[8,2,48,768]{3,2,1,0:T(8,128)(2,1)S(1)}, u32[]{:S(2)}, u32[]{:S(2)}) %all-to-all-start.4) | async-done | bytes 1179680 | tf_op jit(solution)/shard_map/all_to_all | solution.py:18
  101.6 0.4 shard_map.114
  102.0 11.7 %all_to_all.34.pieces_ref = bf16[8,24,384]{2,1,0:T(8,128)(2,1)S(1)} all-to-all(bf16[8,24,384]{2,1,0:T(8,128)(2,1)S(1)} %shard_map.114), channel_id=1, replica_groups=mesh['zl'=2,'y'=8,'x'=4,'zh'=4,'c'=2] {'y'}, dimensions={0} | all-to-all | bytes 294912 | tf_op jit(solution)/shard_map/all_to_all | solution.py:18
  113.7 1.0 shard_map.115
  (14 shorter events, 0.4 us)
Async XLA Ops:
  0.6 38.5 %copy-start = (bf16[1,256,768]{2,1,0:T(8,128)(2,1)S(1)}, bf16[1,256,768]{2,1,0:T(8,128)(2,1)}, u32[]{:S(2)}) copy-start(bf16[1,256,768]{2,1,0:T(8,128)(2,1)} %param.11) | copy-start | bytes 1179652
  38.3 0.8 copy-start.1
  80.9 6.0 %copy-start.2 = (bf16[8,1,48,768]{3,2,1,0:T(8,128)(2,1)S(1)}, bf16[8,1,48,768]{3,2,1,0:T(8,128)(2,1)}, u32[]{:S(2)}) copy-start(bf16[8,1,48,768]{3,2,1,0:T(8,128)(2,1)} %copy-done.1) | copy-start | bytes 1769476
  80.9 20.7 %all-to-all-start.4 = ((bf16[8,2,48,768]{3,2,1,0:T(8,128)(2,1)}), bf16[8,2,48,768]{3,2,1,0:T(8,128)(2,1)S(1)}, u32[]{:S(2)}, u32[]{:S(2)}) async-start(bf16[8,2,48,768]{3,2,1,0:T(8,128)(2,1)} %shard_map.112), calls=%async_computation.4 | async-start | bytes 2359296 | tf_op jit(solution)/shard_map/all_to_all | solution.py:18

commit v9 on v8

--- a/solution.py
+++ b/solution.py
@@ -226,7 +226,7 @@
     (near, w_gate, w_up), other, kept_at, sent_at = lax.optimization_barrier(
         (pick(slots, weights, tokens, cotangent, (w_gate, w_up), 8), other, kept_at, sent_at)
     )
-    rows = exchange(on_chip(near_body, (8, 2, 8 * cap, d), BF16, exchange(near, "y")), ("zl", "x"))
+    rows = exchange(on_chip(near_body, (8, 2, 8 * cap, d), BF16, exchange(near, "y")), ("x", "zl"))
     n = 64 * cap
 
     all_rows, all_grads = (rows[:, i].reshape(n, d) for i in range(2))
@@ -251,7 +251,7 @@
     out = dot(hidden, w_down, 0, 0).astype(BF16)
     both = pair(out.reshape(8, 8 * cap, d), full, w_gate, w_up)
     both, slots, weights = lax.optimization_barrier((both, slots, weights))
-    both = exchange(both, ("zl", "x"))
+    both = exchange(both, ("x", "zl"))
 
     grad_gate = dot(all_rows, d_gate, 0, 1).astype(BF16)
     grad_up = dot(all_rows, d_up, 0, 1).astype(BF16)

time: 115 us -> 116 us (level)
  no operation moved by 1% of the time
where the time goes in v9:
time: 116 us; the launch traced here: 115 us
  blocking collectives  86.1 us (74%)
  waiting for transfers between devices  11.3 us (10%)
  starting transfers between devices  6.06 us (5%)
  Pallas kernels  5.14 us (4%)
  matrix products  4.97 us (4%)
    all_to_all x5, blocking collectives, exchange(): return lax.all_to_all(pieces, axes, split_axis=0, concat_axis=0, tiled=True)  81.6 us
    all_to_all x1, waiting for transfers between devices, exchange(): return lax.all_to_all(pieces, axes, split_axis=0, concat_axis=0, tiled=True)  11.3 us
    all_to_all x1, starting transfers between devices, exchange(): return lax.all_to_all(pieces, axes, split_axis=0, concat_axis=0, tiled=True)  6.06 us
    dot_general x7, matrix products, dot(): lax.dot_general(a, b, (((ca,), (cb,)), ((), ())), preferred_element_type=...  4.97 us
  transfers between devices with their start and end apart: 1, of which 1 were waited for; matrix products, arithmetic and copies ran while one was open for 3% of the time, Pallas kernels for 1%

profile of v9, /device:TPU:6, one launch (start us, length us, event | category | flops | bytes accessed | tf_op | source)
XLA Modules:
  0.0 114.9 jit_solution(11412193850814150772)
XLA Ops:
  0.7 1.4 %shard_map.110 = (bf16[8,24,384]{2,1,0:T(8,128)(2,1)S(1)}, bf16[768,256]{1,0:T(8,128)(2,1)S(1)}, bf16[768,256]{1,0:T(8,128)(2,1)S(1)}) custom-call(s32[6]{0:T(128)} %bitcast.87, f32[6]{0:T(128)} %bitcast.89, bf16[128,768]{1,0:T(8,128)(2,1)} %refs_2_.1, bf16[128,768]{1,0:T(8,128)(2,1)} %refs_3_.1, bf16[768,256]{1,0:T(8,128)(2,1)} %bitcast.82, ...), custom_call_target="tpu_custom_call" | custom-call | tf_op jit(solution)/shard_map/pallas_call | solution.py:159
  2.1 16.3 %all_to_all.30.pieces_ref = bf16[8,24,384]{2,1,0:T(8,128)(2,1)S(1)} all-to-all(bf16[8,24,384]{2,1,0:T(8,128)(2,1)S(1)} %get-tuple-element.31), channel_id=1, replica_groups=mesh['zl'=2,'y'=8,'x'=4,'zh'=4,'c'=2] {'y'}, dimensions={0} | all-to-all | bytes 294912 | tf_op jit(solution)/shard_map/all_to_all | solution.py:18
  18.4 0.2 shard_map.111
  18.6 19.6 %all_to_all.31 = bf16[8,2,48,768]{3,2,1,0:T(8,128)(2,1)S(1)} all-to-all(bf16[8,2,48,768]{3,2,1,0:T(8,128)(2,1)S(1)} %shard_map.111), channel_id=1, replica_groups=mesh['zl'=2,'y'=8,'x'=4,'zh'=4,'c'=2] {'x','zl'}, dimensions={0} | all-to-all | bytes 2359296 | tf_op jit(solution)/shard_map/all_to_all | solution.py:18
  38.3 0.4 convolution_bitcast_fusion.1
  38.7 0.4 convolution_bitcast_fusion.2
  39.1 0.4 convolution_bitcast_fusion
  39.5 0.1 pad_maximum_fusion
  39.7 2.2 %all-gather = bf16[6,128,384]{2,1,0:T(8,128)(2,1)S(1)} all-gather(bf16[3,128,384]{2,1,0:T(8,128)(2,1)S(1)} %dynamic-slice_convert_fusion), channel_id=2, replica_groups=mesh['zl'=2,'y'=8,'x'=4,'zh'=4,'c'=2] {'c'}, dimensions={0}, use_global_device_ids=true | all-gather | bytes 884736 | tf_op jit(solution)/shard_map/all_gather | solution.py:234
  41.9 0.1 fusion
  42.1 21.4 %all_to_all.32 = bf16[4,3,32,384]{3,2,1,0:T(8,128)(2,1)S(1)} all-to-all(bf16[4,3,32,384]{3,2,1,0:T(8,128)(2,1)S(1)} %bitcast.78), channel_id=1, replica_groups=mesh['zl'=2,'y'=8,'x'=4,'zh'=4,'c'=2] {'zh'}, dimensions={0} | all-to-all | bytes 589824 | tf_op jit(solution)/shard_map/all_to_all | solution.py:18
  63.6 12.4 %all_to_all.33 = bf16[4,3,32,384]{3,2,1,0:T(8,128)(2,1)S(1)} all-to-all(bf16[4,3,32,384]{3,2,1,0:T(8,128)(2,1)S(1)} %broadcast_in_dim.15), channel_id=1, replica_groups=mesh['zl'=2,'y'=8,'x'=4,'zh'=4,'c'=2] {'zh'}, dimensions={0} | all-to-all | bytes 589824 | tf_op jit(solution)/shard_map/all_to_all | solution.py:18
  76.0 2.2 %all_gather.11.full_ref = bf16[8,3,32,384]{3,2,1,0:T(8,128)(2,1)S(1)} all-gather(bf16[4,3,32,384]{3,2,1,0:T(8,128)(2,1)S(1)} %all_to_all.33), channel_id=1, replica_groups=mesh['zl'=2,'y'=8,'x'=4,'zh'=4,'c'=2] {'c'}, dimensions={0}, use_global_device_ids=true | all-gather | bytes 884736 | tf_op jit(solution)/shard_map/all_gather | solution.py:248
  78.3 0.4 convolution_convert_fusion
  78.7 1.4 %shard_map.112 = bf16[8,2,48,768]{3,2,1,0:T(8,128)(2,1)} custom-call(bf16[8,48,768]{2,1,0:T(8,128)(2,1)S(1)} %bitcast.68, bf16[8,3,32,384]{3,2,1,0:T(8,128)(2,1)S(1)} %all_gather.11.full_ref, bf16[768,256]{1,0:T(8,128)(2,1)S(1)} %get-tuple-element.30.w_gate_ref, bf16[768,256]{1,0:T(8,128)(2,1)S(1)} %get-tuple-element.32.w_up_ref), custom_call_target="tpu_custom_call" | custom-call | tf_op jit(solution)/shard_map/pallas_call | solution.py:185
  80.1 6.1 %all-to-all-start.4 = ((bf16[8,2,48,768]{3,2,1,0:T(8,128)(2,1)}), bf16[8,2,48,768]{3,2,1,0:T(8,128)(2,1)S(1)}, u32[]{:S(2)}, u32[]{:S(2)}) async-start(bf16[8,2,48,768]{3,2,1,0:T(8,128)(2,1)} %shard_map.112), calls=%async_computation.4 | async-start | bytes 2359296 | tf_op jit(solution)/shard_map/all_to_all | solution.py:18
  86.2 0.7 shard_map.113
  86.9 1.1 convolution_convert_fusion.1
  88.0 1.2 %convolution_convert_fusion.3 = bf16[768,256]{1,0:T(8,128)(2,1)} fusion(bf16[384,768]{1,0:T(8,128)(2,1)S(1)} %bitcast.71, bf16[256,384]{1,0:T(8,128)(2,1)S(1)} %bitcast.81), kind=kOutput, calls=%fused_computation.3 | convolution fusion | flops 151191552 | bytes 1179648 | tf_op jit(solution)/shard_map/dot_general | solution.py:33
  89.2 1.2 %convolution_convert_fusion.2 = bf16[768,256]{1,0:T(8,128)(2,1)} fusion(bf16[384,768]{1,0:T(8,128)(2,1)S(1)} %bitcast.72, bf16[256,384]{1,0:T(8,128)(2,1)S(1)} %bitcast.80), kind=kOutput, calls=%fused_computation.2 | convolution fusion | flops 151191552 | bytes 1179648 | tf_op jit(solution)/shard_map/dot_general | solution.py:33
  90.3 11.3 %all-to-all-done.4.pieces_ref = bf16[8,2,48,768]{3,2,1,0:T(8,128)(2,1)S(1)} async-done(((bf16[8,2,48,768]{3,2,1,0:T(8,128)(2,1)}), bf16[8,2,48,768]{3,2,1,0:T(8,128)(2,1)S(1)}, u32[]{:S(2)}, u32[]{:S(2)}) %all-to-all-start.4) | async-done | bytes 1179680 | tf_op jit(solution)/shard_map/all_to_all | solution.py:18
  101.6 0.4 shard_map.114
  102.0 11.9 %all_to_all.34.pieces_ref = bf16[8,24,384]{2,1,0:T(8,128)(2,1)S(1)} all-to-all(bf16[8,24,384]{2,1,0:T(8,128)(2,1)S(1)} %shard_map.114), channel_id=1, replica_groups=mesh['zl'=2,'y'=8,'x'=4,'zh'=4,'c'=2] {'y'}, dimensions={0} | all-to-all | bytes 294912 | tf_op jit(solution)/shard_map/all_to_all | solution.py:18
  113.9 1.0 shard_map.115
  (14 shorter events, 0.4 us)
Async XLA Ops:
  0.6 38.5 %copy-start = (bf16[1,256,768]{2,1,0:T(8,128)(2,1)S(1)}, bf16[1,256,768]{2,1,0:T(8,128)(2,1)}, u32[]{:S(2)}) copy-start(bf16[1,256,768]{2,1,0:T(8,128)(2,1)} %param.11) | copy-start | bytes 1179652
  38.3 0.8 copy-start.1
  80.1 6.8 %copy-start.2 = (bf16[8,1,48,768]{3,2,1,0:T(8,128)(2,1)S(1)}, bf16[8,1,48,768]{3,2,1,0:T(8,128)(2,1)}, u32[]{:S(2)}) copy-start(bf16[8,1,48,768]{3,2,1,0:T(8,128)(2,1)} %copy-done.1) | copy-start | bytes 1769476
  80.1 21.5 %all-to-all-start.4 = ((bf16[8,2,48,768]{3,2,1,0:T(8,128)(2,1)}), bf16[8,2,48,768]{3,2,1,0:T(8,128)(2,1)S(1)}, u32[]{:S(2)}, u32[]{:S(2)}) async-start(bf16[8,2,48,768]{3,2,1,0:T(8,128)(2,1)} %shard_map.112), calls=%async_computation.4 | async-start | bytes 2359296 | tf_op jit(solution)/shard_map/all_to_all | solution.py:18
